TPU v7x, 128 devices: a whole 4x4x4 slice. The times are simulated.
128 devices in a mesh: tm: 32 (over z, y, core), rep: 4 (over x).
Axes of the slice: x: 4, y: 4, z: 4, core: 2. Of those that a mesh axis runs over, the one named last changes fastest.
Arguments:
- transitions: float32 [128, 512, 512], P(('rep', 'tm')), parts along dimension 0, may hold values from -1 to 1, as said below
- cond_covs: float32 [128, 512, 512], P(('rep', 'tm')), parts along dimension 0, may hold values from -40 to 40, as said below
- transition_est: float32 [2048, 512], P('rep'), parts along dimension 0, may hold values from -0.25 to 0.25
Outputs:
- cov_blocks: float32 [128, 512, 512], P(('rep', 'tm')), parts along dimension 0
- transition_grad: float32 [2048, 512], P('rep'), parts along dimension 0
There are 4 independent parts, one for each index of `rep`. A program takes and returns all parts, laid end to end along the dimension named above; each array names one. Nothing has to cross between parts.
Inputs may be any that keep to these rules, and one draw needn't show every extreme that they name: `transitions`: every block has spectral norm below one. `cond_covs`: every block is symmetric and positive definite.
All inputs are finite; a program needn't handle non-finite values.
Results may differ from a plain program's by a relative error of at most 0.00017.
Values sent between devices are 32-bit elements; how exact they have to be, the bound alone decides.
No kernel may reach another device: no remote copies, remote signals or barrier semaphores. Data moves between devices by JAX's collectives and lax.ppermute only.
A program may use at most 192 MiB of HBM per device.

v0:
```python
import jax
import jax.numpy as jnp
from jax import lax
from jax.sharding import PartitionSpec as P

highest = lax.Precision.HIGHEST


def entering(part, axis, combine, identity):
    count = lax.axis_size(axis)
    place = lax.axis_index(axis)
    ahead = count - 1 - place
    gathered = jax.tree.map(lambda a: lax.all_gather(a, axis), part)
    state = jax.tree.map(lambda a, e: jnp.zeros_like(a) + jnp.asarray(e, a.dtype), part, identity)

    def one(step, state):
        source = count - 1 - step
        return combine(
            state, jax.tree.map(lambda a: lax.dynamic_index_in_dim(a, source, 0, False), gathered)
        )

    return lax.fori_loop(0, ahead, one, state)


def times_transposed(left, right):
    return lax.dot_general(
        left, right, (((1,), (1,)), ((), ())), precision=highest, preferred_element_type=jnp.float32
    )


def product(left, right):
    return jnp.dot(left, right, precision=highest, preferred_element_type=jnp.float32)


def compose(earlier, latter):
    gain_first, noise_first = earlier
    gain_second, second_noise = latter
    combined_gain = product(gain_second, gain_first)
    combined_noise = product(gain_second, times_transposed(noise_first, gain_second)) + second_noise
    return (combined_gain, combined_noise)


def on_device(transitions, cond_covs, transition_est):
    blocks_here = transitions.shape[0]
    width = transitions.shape[1]
    devices = lax.axis_size("tm")
    total_blocks = blocks_here * devices
    position = lax.axis_index("tm")
    combined_gain = transitions[blocks_here - 1]
    combined_noise = cond_covs[blocks_here - 1]
    empty_block = jnp.zeros((width, width), jnp.float32)
    identity = jnp.eye(width, dtype=jnp.float32)
    prefix = entering((combined_gain, combined_noise), "tm", compose, (identity, empty_block))
    covariance = prefix[1]
    transition = transitions[0]
    previous_step_cross = times_transposed(covariance, transition)
    covariance = product(transition, previous_step_cross) + cond_covs[0]
    collected = [covariance]
    current_entry = jnp.where(position * blocks_here + 0 < total_blocks - 1, 1.0, 0.0).astype(
        jnp.float32
    )
    accumulated = current_entry * (previous_step_cross - product(transition_est, covariance))
    gradient = lax.psum(accumulated, "tm") / (total_blocks - 1)
    cov_blocks = jnp.stack(collected[::-1], axis=0)
    return (cov_blocks, gradient)


def solution(mesh):
    return jax.shard_map(
        on_device,
        mesh=mesh,
        in_specs=(P(("rep", "tm"), None, None), P(("rep", "tm"), None, None), P("rep", None)),
        out_specs=(P(("rep", "tm"), None, None), P("rep", None)),
        check_vma=False,
    )
```

profile of v0, /device:TPU:1, one launch (start us, length us, event | category | flops | bytes accessed | tf_op | source)
XLA Modules:
  0.0 565.4 jit_solution(15440725541577680220)
XLA Ops:
  11.3 116.7 %all-gather.3.cloned.1.call-done = f32[32,512,512]{2,1,0:T(8,128)} async-done(((f32[1,512,512]{2,1,0:T(8,128)}), f32[32,512,512]{2,1,0:T(8,128)}) %all-gather.3.cloned.1.call-update) | async-done | bytes 33554448 | tf_op jit(solution)/shard_map/all_gather | solution.py:13
  127.9 115.5 %all-gather.5.cloned.1.call-done = f32[32,512,512]{2,1,0:T(8,128)} async-done(((f32[1,512,512]{2,1,0:T(8,128)}), f32[32,512,512]{2,1,0:T(8,128)}) %all-gather.5.cloned.1.call-update) | async-done | bytes 33554448 | tf_op jit(solution)/shard_map/all_gather | solution.py:13
  243.5 196.2 %while.14 = (s32[]{:T(128)}, f32[512,512]{1,0:T(8,128)S(1)}, s32[]{:T(128)}, f32[32,512,512]{2,1,0:T(8,128)}, f32[32,512,512]{2,1,0:T(8,128)}, /*index=5*/s32[]{:T(128)}, s32[]{:T(128)}, s32[]{:T(128)}, s32[]{:T(128)}) while((s32[]{:T(128)}, f32[512,512]{1,0:T(8,128)S(1)}, s32[]{:T(128)}, f32[32,512,512]{2,1,0:T(8,128)}, ...), condition=%wide.region_1.2_spmd, body=%wide.region_0.1_spmd.sunk | while | flops 3221487616 | bytes 7341199 | solution.py:22
  243.5 3.1 fusion.28
  246.6 3.4 convolution_add_fusion.2
  250.1 3.1 fusion.28
  253.2 3.4 convolution_add_fusion.2
  256.6 3.1 fusion.28
  259.7 3.4 convolution_add_fusion.2
  263.1 3.1 fusion.28
  266.2 3.4 convolution_add_fusion.2
  269.7 3.1 fusion.28
  272.8 3.4 convolution_add_fusion.2
  276.2 3.1 fusion.28
  279.3 3.4 convolution_add_fusion.2
  282.7 3.1 fusion.28
  285.8 3.4 convolution_add_fusion.2
  289.3 3.1 fusion.28
  292.4 3.4 convolution_add_fusion.2
  295.8 3.1 fusion.28
  298.9 3.4 convolution_add_fusion.2
  302.3 3.1 fusion.28
  305.4 3.4 convolution_add_fusion.2
  308.9 3.1 fusion.28
  312.0 3.4 convolution_add_fusion.2
  315.4 3.1 fusion.28
  318.5 3.4 convolution_add_fusion.2
  321.9 3.1 fusion.28
  325.0 3.4 convolution_add_fusion.2
  328.5 3.1 fusion.28
  331.6 3.4 convolution_add_fusion.2
  335.0 3.1 fusion.28
  338.1 3.4 convolution_add_fusion.2
  341.5 3.1 fusion.28
  344.6 3.4 convolution_add_fusion.2
  348.1 3.1 fusion.28
  351.2 3.4 convolution_add_fusion.2
  354.6 3.1 fusion.28
  357.7 3.4 convolution_add_fusion.2
  361.1 3.1 fusion.28
  364.2 3.4 convolution_add_fusion.2
  367.7 3.1 fusion.28
  370.8 3.4 convolution_add_fusion.2
  374.2 3.1 fusion.28
  377.3 3.4 convolution_add_fusion.2
  380.8 3.1 fusion.28
  383.8 3.4 convolution_add_fusion.2
  387.3 3.1 fusion.28
  390.4 3.4 convolution_add_fusion.2
  393.8 3.1 fusion.28
  396.9 3.4 convolution_add_fusion.2
  400.4 3.1 fusion.28
  403.5 3.4 convolution_add_fusion.2
  406.9 3.1 fusion.28
  410.0 3.4 convolution_add_fusion.2
  413.4 3.1 fusion.28
  416.5 3.4 convolution_add_fusion.2
  423.1 3.4 convolution_add_fusion.2
  426.5 3.1 fusion.28
  429.6 3.4 convolution_add_fusion.2
  433.0 3.1 fusion.28
  436.1 3.4 convolution_add_fusion.2
  441.6 4.7 fusion.9
  450.5 106.1 %all-reduce.2.cloned.1.call-done = f32[512,512]{1,0:T(8,128)} async-done(((f32[512,512]{1,0:T(8,128)}), f32[512,512]{1,0:T(8,128)}) %all-reduce.2.cloned.1.call-update) | async-done | bytes 1048592 | tf_op jit(solution)/shard_map/psum | solution.py:63
  (17 shorter events, 15.6 us)
Async XLA Ops:
  7.2 439.2 %copy-start = (f32[512,512]{1,0:T(8,128)S(1)}, f32[512,512]{1,0:T(8,128)}, u32[]{:S(2)}) copy-start(f32[512,512]{1,0:T(8,128)} %param.7) | copy-start | bytes 3145732
  7.2 432.6 %copy-start.1 = (f32[1,512,512]{2,1,0:T(8,128)S(1)}, f32[1,512,512]{2,1,0:T(8,128)}, u32[]{:S(2)}) copy-start(f32[1,512,512]{2,1,0:T(8,128)} %param.5) | copy-start | bytes 3145732
  7.2 120.7 %all-gather.3.cloned.1.call-start = ((), (), s32[]{:S(2)}) async-start(), calls=%async_computation | async-start | bytes 34603008 | tf_op jit(solution)/shard_map/all_gather | solution.py:13
  7.9 235.5 %all-gather.5.cloned.1.call-start = ((), (), s32[]{:S(2)}) async-start(), calls=%async_computation.1 | async-start | bytes 34603008 | tf_op jit(solution)/shard_map/all_gather | solution.py:13
  8.7 547.9 %all-reduce.2.cloned.1.call-start = ((), (), s32[]{:S(2)}) async-start(), calls=%async_computation.2 | async-start | bytes 2097152 | tf_op jit(solution)/shard_map/psum | solution.py:63
Sparse Core Ops, SparseCore 0:
  10.3 117.5 all-gather.2
  130.2 113.1 all-gather.4
  449.3 107.2 all-reduce.1
where the time goes:
time: 568 us; the launch traced here: 565 us
  waiting for transfers between devices  340 us (60%)
  matrix products  204 us (36%)
  between operations  13.8 us (2%)
    all_gather x2, waiting for transfers between devices, entering(): gathered = jax.tree.map(lambda a: lax.all_gather(a, axis), part)  232 us
    dot_general x32, matrix products, product(): jnp.dot(left, right, precision=highest, preferred_element_type=jnp.float32)  110 us
    psum x1, waiting for transfers between devices, on_device(): gradient = lax.psum(accumulated, 'tm') / (total_blocks - 1)  106 us
    dot_general x31, matrix products, times_transposed(): lax.dot_general(left, right, (((1,), (1,)), ((), ())), precision=highest,...  94.5 us
  transfers between devices with their start and end apart: 3, of which 3 were waited for; matrix products, arithmetic and copies ran while one was open for 1% of the time, Pallas kernels for 0%

commit v1 on v0

v1 whole, which is shorter than its diff:
```python
import jax
import jax.numpy as jnp
from jax import lax
from jax.experimental import pallas as pl
from jax.experimental.pallas import tpu as pltpu
from jax.sharding import PartitionSpec as P

ROWS = 4
CHIPS = 4
CORES = 2
PAD = 8
VMEM_LIMIT = 24 * 2**20


def device(z, y, core):
    return ((z % ROWS) * CHIPS + y % CHIPS) * CORES + core


def moved(x, source):
    pairs = []
    for z in range(ROWS):
        for y in range(CHIPS):
            for c in range(CORES):
                origin = source(z, y, c)
                if origin is not None:
                    pairs.append((device(*origin), device(z, y, c)))
    return lax.ppermute(x, "tm", pairs)


def swap_cores(x):
    return moved(x, lambda z, y, c: (z, y, 1 - c))


def from_chip_ahead(x, distance):
    return moved(x, lambda z, y, c: (z, y + distance, c))


def from_row_ahead(x, distance, rows=tuple(range(ROWS))):
    return moved(x, lambda z, y, c: (z + distance, y, c) if z in rows else None)


def place():
    here = lax.axis_index("tm")
    return here // (CHIPS * CORES), (here // CORES) % CHIPS, here % CORES


def split(x):
    high = x.astype(jnp.bfloat16)
    return high, (x - high.astype(jnp.float32)).astype(jnp.bfloat16)


def dot3(left, right, contract=0):
    def one(a, b):
        return lax.dot_general(
            a, b, (((1,), (contract,)), ((), ())), preferred_element_type=jnp.float32
        )

    (left_high, left_low), (right_high, right_low) = left, right
    return one(left_low, right_high) + one(left_high, right_low) + one(left_high, right_high)


def carry(gain, cov, noise):
    return noise + dot3(split(dot3(gain, split(cov))), gain, 1)


def kernel_call(body, shapes, operands, scratch=(), flops=0, moved_bytes=0):
    vmem = pl.BlockSpec(memory_space=pltpu.VMEM)
    return pl.pallas_call(
        body,
        out_shape=[jax.ShapeDtypeStruct(shape, jnp.float32) for shape in shapes],
        in_specs=[vmem] * len(operands),
        out_specs=[vmem] * len(shapes),
        scratch_shapes=[pltpu.VMEM(shape, jnp.float32) for shape in scratch],
        compiler_params=pltpu.CompilerParams(vmem_limit_bytes=VMEM_LIMIT),
        cost_estimate=pl.CostEstimate(flops=flops, bytes_accessed=moved_bytes, transcendentals=0),
    )(*operands)


def rows_at(index, size):
    return pl.ds(pl.multiple_of(index * size, size), size)


def triangles(half):
    rows = lax.broadcasted_iota(jnp.int32, (half, half), 0)
    columns = lax.broadcasted_iota(jnp.int32, (half, half), 1)
    return rows >= columns, rows == columns


def pack(x, out_ref, start, core):
    half = x.shape[0] // 2
    quarter = half // 2
    lower, on_diagonal = triangles(half)
    a, b, d = x[:half, :half], x[:half, half:], x[half:, half:]
    diagonal = jnp.sum(jnp.where(on_diagonal, d, 0.0), axis=0, keepdims=True)
    w = jnp.where(core == 0, jnp.where(lower, a, d), b)
    out_ref[start : start + quarter, :half] = w[:quarter]
    out_ref[start : start + quarter, half:] = w[quarter:]
    out_ref[start + quarter : start + quarter + PAD, :half] = jnp.broadcast_to(diagonal, (PAD, half))
    out_ref[start + quarter : start + quarter + PAD, half:] = jnp.broadcast_to(diagonal, (PAD, half))


def unpack(mine, other, core):
    half = mine.shape[1] // 2
    quarter = half // 2
    lower, on_diagonal = triangles(half)

    def square(x):
        return jnp.concatenate([x[:quarter, :half], x[:quarter, half:]], axis=0)

    diagonal = jnp.where(core == 0, mine, other)[quarter : quarter + 1, :half]
    mine, other = square(mine), square(other)
    w = jnp.where(core == 0, mine, other)
    b = jnp.where(core == 0, other, mine)
    flipped = w.T
    a = jnp.where(lower, w, flipped)
    d = jnp.where(on_diagonal, diagonal, jnp.where(lower, flipped, w))
    top = jnp.concatenate([a, b], axis=1)
    return jnp.concatenate([top, jnp.concatenate([b.T, d], axis=1)], axis=0)


def chip_kernel(gain, gain_other, noise, noise_other, gain_ref, noise_ref, send_ref, g_ref, n_ref):
    _, _, core = place()
    half = gain.shape[0] // 2
    g_ref[core], g_ref[1 - core] = gain[...], gain_other[...]
    n_ref[core], n_ref[1 - core] = noise[...], noise_other[...]
    first = split(g_ref[0])
    gain_ref[...] = dot3(first, split(g_ref[1]))
    send_ref[:half] = gain_ref[rows_at(core, half), :]
    result = carry(first, n_ref[1], n_ref[0])
    noise_ref[...] = result
    pack(result, send_ref, half, core)


def row_kernel(own_gain, own_noise, *refs):
    ahead, ahead_other, behind, behind_other, far, far_other, rest, rest_other = refs[:8]
    after_gain_ref, after_noise_ref, gain_ref, gain_mine_ref, noise_ref, packed_ref, p_ref, n_ref = refs[8:]
    _, y, core = place()
    width = own_gain.shape[0]
    half = width // 2
    p_ref[y], n_ref[y] = own_gain[...], own_noise[...]
    for slot, mine, other in (
        ((y + 1) % CHIPS, ahead, ahead_other),
        ((y + 3) % CHIPS, behind, behind_other),
    ):
        p_ref[slot, rows_at(core, half), :] = mine[:half]
        p_ref[slot, rows_at(1 - core, half), :] = other[:half]
        n_ref[slot] = unpack(mine[half:], other[half:], core)
    slot = (y + 2) % CHIPS
    cut = far.shape[0]
    left = half - cut
    for place_of, upper, lower in ((core, far, rest), (1 - core, far_other, rest_other)):
        start = pl.multiple_of(place_of * half, half)
        p_ref[slot, pl.ds(start, cut), :] = upper[...]
        p_ref[slot, pl.ds(pl.multiple_of(start + cut, 8), left), :] = lower[:left]
    n_ref[slot] = unpack(rest[left:], rest_other[left:], core)

    gain, noise = p_ref[CHIPS - 1], n_ref[CHIPS - 1]

    @pl.when(y == CHIPS - 1)
    def _():
        rows = lax.broadcasted_iota(jnp.int32, (width, width), 0)
        columns = lax.broadcasted_iota(jnp.int32, (width, width), 1)
        after_gain_ref[...] = jnp.where(rows == columns, 1.0, 0.0)
        after_noise_ref[...] = jnp.zeros_like(after_noise_ref)

    for k in range(CHIPS - 2, -1, -1):
        @pl.when(y == k)
        def _(gain=gain, noise=noise):
            after_gain_ref[...] = gain
            after_noise_ref[...] = noise

        step = split(p_ref[k])
        gain = dot3(step, split(gain))
        noise = carry(step, noise, n_ref[k])
    gain_ref[...], noise_ref[...] = gain, noise
    gain_mine_ref[...] = gain_ref[rows_at(core, half), :]
    pack(noise, packed_ref, 0, core)


def after_kernel(
    after_gain, after_noise, gain, gain_other, noise, noise_other, estimate,
    from_gain_ref, from_noise_ref, grad_gain_ref, grad_noise_ref, g_ref, n_ref,
):
    _, _, core = place()

    @pl.when(core == 0)
    def _():
        other = split(gain_other[...])
        g_ref[...] = dot3(other, split(after_gain[...]))
        n_ref[...] = carry(other, after_noise[...], noise_other[...])

    @pl.when(core != 0)
    def _():
        g_ref[...] = after_gain[...]
        n_ref[...] = after_noise[...]

    own, transition = split(gain[...]), split(estimate[...])
    from_gain = dot3(own, split(g_ref[...]))
    from_gain_ref[...] = from_gain
    grad_gain_ref[...] = g_ref[...] - dot3(transition, split(from_gain))
    lagged = dot3(split(n_ref[...]), own, 1)
    from_noise = dot3(own, split(lagged)) + noise[...]
    from_noise_ref[...] = from_noise
    grad_noise_ref[...] = lagged - dot3(transition, split(from_noise))


def next_row_kernel(mine, other, gain, noise, next_ref, packed_ref):
    _, _, core = place()
    following = unpack(mine[...], other[...], core)
    next_ref[...] = following
    pack(carry(split(gain[...]), following, noise[...]), packed_ref, 0, core)


def final_kernel(
    near, near_other, far, far_other, mine, other, following, from_gain, from_noise, grad_gain, grad_noise,
    cov_ref, keep_ref, give_ref, t_ref, g_ref,
):
    z, y, core = place()
    half = mine.shape[0]

    @pl.when(z == 0)
    def _():
        g_ref[rows_at(core, half), :] = mine[...]
        g_ref[rows_at(1 - core, half), :] = other[...]
        second = unpack(far[...], far_other[...], core)
        t_ref[...] = carry(split(g_ref[...]), second, following[...])

    @pl.when(z == 1)
    def _():
        t_ref[...] = unpack(near[...], near_other[...], core)

    @pl.when(z == 2)
    def _():
        t_ref[...] = following[...]

    @pl.when(z == 3)
    def _():
        t_ref[...] = jnp.zeros_like(t_ref)

    gain = split(from_gain[...])
    carried = split(dot3(split(t_ref[...]), gain, 1))
    last = (z == ROWS - 1) & (y == CHIPS - 1) & (core == CORES - 1)
    terms = jnp.where(last, 0.0, grad_noise[...] + dot3(split(grad_gain[...]), carried))
    cov_ref[...] = from_noise[...] + dot3(gain, carried)

    @pl.when(core == 0)
    def _():
        keep_ref[...], give_ref[...] = terms[:half], terms[half:]

    @pl.when(core != 0)
    def _():
        keep_ref[...], give_ref[...] = terms[half:], terms[:half]


def share_kernel(keep, given, *refs):
    outs, total_ref = refs[:CHIPS], refs[CHIPS]
    _, y, _ = place()
    total_ref[...] = keep[...] + given[...]
    for r in range(CHIPS):
        outs[r][...] = total_ref[rows_at((y + r) % CHIPS, outs[r].shape[0]), :]


def sum_kernel(a, b, c, d, out_ref):
    out_ref[...] = (a[...] + b[...]) + (c[...] + d[...])


def total_kernel(count, a, b, c, d, out_ref, z_ref):
    z, _, _ = place()
    for r, piece in enumerate((a, b, c, d)):
        z_ref[(z + r) % ROWS] = piece[...]
    out_ref[...] = ((z_ref[0] + z_ref[1]) + (z_ref[2] + z_ref[3])) / count


def half_kernel(a, b, c, d, out_ref):
    _, y, _ = place()
    for r, piece in enumerate((a, b, c, d)):
        out_ref[rows_at((y + r) % CHIPS, piece.shape[0]), :] = piece[...]


def whole_kernel(mine, other, out_ref):
    _, _, core = place()
    half = mine.shape[0]
    out_ref[rows_at(core, half), :] = mine[...]
    out_ref[rows_at(1 - core, half), :] = other[...]


def on_device(transitions, cond_covs, transition_est):
    gain, noise = transitions[0], cond_covs[0]
    width = gain.shape[0]
    half = width // 2
    square, strip, piece = (width, width), (half, width), (half // 2 + PAD, width)
    chunk = (half // CHIPS, width)
    flops = 6 * width**3
    size = 4 * width * width

    with jax.named_scope("T_chip"):
        gain_other, noise_other = swap_cores(gain), swap_cores(noise)
        chip_gain, chip_noise, mine = kernel_call(
            chip_kernel,
            [square, square, (half + half // 2 + PAD, width)],
            (gain, gain_other, noise, noise_other),
            [(CORES, *square)] * 2,
            3 * flops,
            7 * size,
        )

    with jax.named_scope("T_row"):
        cut = mine.shape[0] // 16 * 8 + 8
        ahead, behind = from_chip_ahead(mine, 1), from_chip_ahead(mine, 3)
        far, rest = from_chip_ahead(ahead[:cut], 1), from_chip_ahead(behind[cut:], 3)
        pieces = []
        for x in (ahead, behind, far, rest):
            pieces += [x, swap_cores(x)]
        after_gain, after_noise, row_gain, row_gain_mine, row_noise, row_packed = kernel_call(
            row_kernel,
            [square, square, square, strip, square, piece],
            (chip_gain, chip_noise, *pieces),
            [(CHIPS, *square)] * 2,
            9 * flops,
            13 * size,
        )

    with jax.named_scope("T_z"):
        next_mine = from_row_ahead(row_packed, 1, (0, 2))
        gain_mine = from_row_ahead(row_gain_mine, 1, (0,))
        parts = kernel_call(
            after_kernel,
            [square] * 4,
            (after_gain, after_noise, gain, gain_other, noise, noise_other, transition_est),
            [square] * 2,
            8 * flops,
            11 * size,
        )
        next_mine, *parts = lax.optimization_barrier((next_mine, *parts))
        from_gain, from_noise, grad_gain, grad_noise = parts
        next_noise, second_packed = kernel_call(
            next_row_kernel,
            [square, piece],
            (next_mine, swap_cores(next_mine), row_gain, row_noise),
            (),
            2 * flops,
            4 * size,
        )
        near, far = from_row_ahead(second_packed, 1, (1,)), from_row_ahead(second_packed, 2, (0,))
        covariance, keep, give = kernel_call(
            final_kernel,
            [square, strip, strip],
            (
                near, swap_cores(near), far, swap_cores(far), gain_mine, swap_cores(gain_mine), next_noise,
                from_gain, from_noise, grad_gain, grad_noise,
            ),
            [square] * 2,
            5 * flops,
            10 * size,
        )

    with jax.named_scope("T_reduce"):
        own, *sent = kernel_call(
            share_kernel, [chunk] * CHIPS, (keep, swap_cores(give)), [strip], size // 4, size
        )
        received = [from_chip_ahead(sent[r - 1], CHIPS - r) for r in (1, 2, 3)]
        (row_sum,) = kernel_call(sum_kernel, [chunk], (own, *received), (), size // 8, size)
        received = [from_row_ahead(row_sum, r) for r in (1, 2, 3)]
        terms = lax.axis_size("tm") - 1
        (total,) = kernel_call(
            lambda *refs: total_kernel(terms, *refs),
            [chunk],
            (row_sum, *received),
            [(ROWS, *chunk)],
            size // 8,
            size,
        )
        received = [from_chip_ahead(total, r) for r in (1, 2, 3)]
        (gradient_mine,) = kernel_call(half_kernel, [strip], (total, *received), (), size // 8, size)
        (gradient,) = kernel_call(
            whole_kernel, [square], (gradient_mine, swap_cores(gradient_mine)), (), size // 4, 2 * size
        )
    return covariance[None], gradient


def solution(mesh):
    return jax.shard_map(
        on_device,
        mesh=mesh,
        in_specs=(P(("rep", "tm"), None, None), P(("rep", "tm"), None, None), P("rep", None)),
        out_specs=(P(("rep", "tm"), None, None), P("rep", None)),
        check_vma=False,
    )
```

time: 568 us -> 130 us (0.23)
  waiting for transfers between devices: 340 us -> 65.6 us
  matrix products: 204 us -> 0 us
  starting transfers between devices: 0.11 us -> 34.1 us
  Pallas kernels: 0 us -> 26.7 us
  between operations: 13.8 us -> 0.83 us
    all_gather x2 -> x0, waiting for transfers between devices: 232 us -> none  [entering(): gathered = jax.tree.map(lambda a: lax.all_gather(a, axis), part)]
    dot_general x63 -> x0, matrix products: 204 us -> none  [the longest x32 110 us: product(): jnp.dot(left, right, precision=highest, preferred_element_type=jnp.float32)]
    psum x1 -> x0, waiting for transfers between devices: 106 us -> none  [on_device(): gradient = lax.psum(accumulated, 'tm') / (total_blocks - 1)]
    ppermute x0 -> x29, waiting for transfers between devices: none -> 65.6 us  [moved(): return lax.ppermute(x, 'tm', pairs)]
    ppermute x0 -> x29, starting transfers between devices: none -> 34.1 us  [moved(): return lax.ppermute(x, 'tm', pairs)]
    pallas_call x0 -> x10, Pallas kernels: none -> 26.7 us  [kernel_call(): pl.pallas_call(body, out_shape=[jax.ShapeDtypeStruct(shape, jnp.float32)...]
  transfers between devices with their start and end apart: 3 -> 29, of which waited for: 3 -> 20; matrix products, arithmetic and copies ran while one was open for 1% -> 0% of each run, Pallas kernels for 0% -> 5%
where the time goes in v1:
time: 130 us
  waiting for transfers between devices  65.6 us (50%)
  starting transfers between devices  34.1 us (26%)
  Pallas kernels  26.7 us (21%)
  local copies, waits for them, and re-layouts  2.52 us (2%)
    ppermute x29, waiting for transfers between devices, moved(): return lax.ppermute(x, 'tm', pairs)  65.6 us
    ppermute x29, starting transfers between devices, moved(): return lax.ppermute(x, 'tm', pairs)  34.1 us
    pallas_call x10, Pallas kernels, kernel_call(): pl.pallas_call(body, out_shape=[jax.ShapeDtypeStruct(shape, jnp.float32)...  26.7 us
  transfers between devices with their start and end apart: 29, of which 20 were waited for; matrix products, arithmetic and copies ran while one was open for 0% of the time, Pallas kernels for 5%

profile of v1, /device:TPU:1, one launch (start us, length us, event | category | flops | bytes accessed | tf_op | source)
XLA Modules:
  0.0 129.8 jit_solution(6768039561881956249)
XLA Ops:
  0.6 1.5 %collective-permute-start = (f32[512,512]{1,0:T(8,128)}, f32[512,512]{1,0:T(8,128)S(1)}, u32[]{:S(2)}, u32[]{:S(2)}) collective-permute-start(f32[512,512]{1,0:T(8,128)} %bitcast.3), channel_id=1, source_target_pairs={{4,0},{0,4},{12,8},{8,12},{20,16},{16,20},{28,24},{24,28},{36,32},... | collective-permute-start | bytes 3145736 | tf_op jit(solution)/shard_map/T_chip/ppermute | solution.py:27
  2.1 0.1 collective-permute-start.1
  2.2 2.4 %collective-permute-done.gain_other = f32[512,512]{1,0:T(8,128)S(1)} collective-permute-done((f32[512,512]{1,0:T(8,128)}, f32[512,512]{1,0:T(8,128)S(1)}, u32[]{:S(2)}, u32[]{:S(2)}) %collective-permute-start) | collective-permute-done | bytes 1048608 | tf_op jit(solution)/shard_map/T_chip/ppermute | solution.py:27
  4.6 1.5 %collective-permute-done.1.noise_other = f32[512,512]{1,0:T(8,128)S(1)} collective-permute-done((f32[512,512]{1,0:T(8,128)}, f32[512,512]{1,0:T(8,128)S(1)}, u32[]{:S(2)}, u32[]{:S(2)}) %collective-permute-start.1) | collective-permute-done | bytes 1048608 | tf_op jit(solution)/shard_map/T_chip/ppermute | solution.py:27
  6.1 1.2 copy-done
  7.4 1.2 copy-done.2
  8.6 3.4 %T_chip.1 = (f32[512,512]{1,0:T(8,128)S(1)}, f32[512,512]{1,0:T(8,128)S(1)}, f32[392,512]{1,0:T(8,128)S(1)}) custom-call(f32[512,512]{1,0:T(8,128)S(1)} %bitcast.4, f32[512,512]{1,0:T(8,128)S(1)} %collective-permute-done.gain_other, f32[512,512]{1,0:T(8,128)S(1)} %bitcast.7, f32[512,512]{1,0:T(8,128)S(1)} %collective-permute-done.1.noise_other), custom_call_target="tpu_custom_call" | custom-call | flops 2415919104 | bytes 7340032 | tf_op jit(solution)/shard_map/T_chip/pallas_call | solution.py:68
  12.0 2.9 %collective-permute-start.2 = (f32[392,512]{1,0:T(8,128)S(1)}, f32[392,512]{1,0:T(8,128)S(1)}, u32[]{:S(2)}, u32[]{:S(2)}) collective-permute-start(f32[392,512]{1,0:T(8,128)S(1)} %get-tuple-element.31), channel_id=1, source_target_pairs={{8,0},{12,4},{16,8},{20,12},{24,16},{28,20},{0,24},{4,28},{40,32},... | collective-permute-start | bytes 2408456 | tf_op jit(solution)/shard_map/T_row/ppermute | solution.py:27
  14.9 16.9 %collective-permute-done.2.refs_0_ = f32[392,512]{1,0:T(8,128)S(1)} collective-permute-done((f32[392,512]{1,0:T(8,128)S(1)}, f32[392,512]{1,0:T(8,128)S(1)}, u32[]{:S(2)}, u32[]{:S(2)}) %collective-permute-start.2) | collective-permute-done | bytes 802848 | tf_op jit(solution)/shard_map/T_row/ppermute | solution.py:27
  31.8 3.5 %collective-permute-start.6 = (f32[200,512]{1,0:T(8,128)S(1)}, f32[200,512]{1,0:T(8,128)S(1)}, u32[]{:S(2)}, u32[]{:S(2)}) collective-permute-start(f32[200,512]{1,0:T(8,128)S(1)} %slice.8), channel_id=1, source_target_pairs={{8,0},{12,4},{16,8},{20,12},{24,16},{28,20},{0,24},{4,28},{40,32},... | collective-permute-start | bytes 1228808 | tf_op jit(solution)/shard_map/T_row/ppermute | solution.py:27
  35.3 1.5 %collective-permute-start.5 = (f32[392,512]{1,0:T(8,128)S(1)}, f32[392,512]{1,0:T(8,128)S(1)}, u32[]{:S(2)}, u32[]{:S(2)}) collective-permute-start(f32[392,512]{1,0:T(8,128)S(1)} %collective-permute-done.4.refs_2_), channel_id=1, source_target_pairs={{4,0},{0,4},{12,8},{8,12},{20,16},{16,20},{28,24},{24,28},{36,32},... | collective-permute-start | bytes 2408456 | tf_op jit(solution)/shard_map/T_row/ppermute | solution.py:27
  36.8 0.0 collective-permute-start.3
  36.8 0.1 collective-permute-start.8
  36.9 5.9 %collective-permute-done.6.refs_4_ = f32[200,512]{1,0:T(8,128)S(1)} collective-permute-done((f32[200,512]{1,0:T(8,128)S(1)}, f32[200,512]{1,0:T(8,128)S(1)}, u32[]{:S(2)}, u32[]{:S(2)}) %collective-permute-start.6) | collective-permute-done | bytes 409632 | tf_op jit(solution)/shard_map/T_row/ppermute | solution.py:27
  42.8 2.1 %collective-permute-start.7 = (f32[200,512]{1,0:T(8,128)S(1)}, f32[200,512]{1,0:T(8,128)S(1)}, u32[]{:S(2)}, u32[]{:S(2)}) collective-permute-start(f32[200,512]{1,0:T(8,128)S(1)} %collective-permute-done.6.refs_4_), channel_id=1, source_target_pairs={{4,0},{0,4},{12,8},{8,12},{20,16},{16,20},{28,24},{24,28},{36,32},... | collective-permute-start | bytes 1228808 | tf_op jit(solution)/shard_map/T_row/ppermute | solution.py:27
  44.9 3.3 %collective-permute-done.8.refs_6_ = f32[192,512]{1,0:T(8,128)S(1)} collective-permute-done((f32[192,512]{1,0:T(8,128)S(1)}, f32[192,512]{1,0:T(8,128)S(1)}, u32[]{:S(2)}, u32[]{:S(2)}) %collective-permute-start.8) | collective-permute-done | bytes 393248 | tf_op jit(solution)/shard_map/T_row/ppermute | solution.py:27
  48.2 1.4 %collective-permute-start.9 = (f32[192,512]{1,0:T(8,128)S(1)}, f32[192,512]{1,0:T(8,128)S(1)}, u32[]{:S(2)}, u32[]{:S(2)}) collective-permute-start(f32[192,512]{1,0:T(8,128)S(1)} %collective-permute-done.8.refs_6_), channel_id=1, source_target_pairs={{4,0},{0,4},{12,8},{8,12},{20,16},{16,20},{28,24},{24,28},{36,32},... | collective-permute-start | bytes 1179656 | tf_op jit(solution)/shard_map/T_row/ppermute | solution.py:27
  49.6 1.3 %collective-permute-done.9.refs_7_ = f32[192,512]{1,0:T(8,128)S(1)} collective-permute-done((f32[192,512]{1,0:T(8,128)S(1)}, f32[192,512]{1,0:T(8,128)S(1)}, u32[]{:S(2)}, u32[]{:S(2)}) %collective-permute-start.9) | collective-permute-done | bytes 393248 | tf_op jit(solution)/shard_map/T_row/ppermute | solution.py:27
  51.0 0.0 collective-permute-done.5.refs_3_
  51.0 0.0 collective-permute-done.3.refs_1_
  51.0 0.0 collective-permute-done.7.refs_5_
  51.0 0.0 copy-start.1
  51.0 0.0 copy-start.3
  51.0 0.0 copy-start.4
  51.0 9.5 %T_row.1 = (f32[512,512]{1,0:T(8,128)S(1)}, f32[512,512]{1,0:T(8,128)S(1)}, f32[512,512]{1,0:T(8,128)S(1)}, f32[256,512]{1,0:T(8,128)S(1)}, f32[512,512]{1,0:T(8,128)S(1)}, /*index=5*/f32[136,512]{1,0:T(8,128)S(1)}) custom-call(f32[512,512]{1,0:T(8,128)S(1)} %get-tuple-element.29.own_gain, f32[512,512]{1,0:T(8,128)S(1)} %get-tuple-element.30.own_noise, ...), custom_call_target="tpu_custom_call" | custom-call | flops 7247757312 | bytes 13631488 | tf_op jit(solution)/shard_map/T_row/pallas_call | solution.py:68
  60.5 1.3 collective-permute-start.10
  61.8 1.3 collective-permute-start.16
  63.1 4.6 %T_z.3 = (f32[512,512]{1,0:T(8,128)S(1)}, f32[512,512]{1,0:T(8,128)S(1)}, f32[512,512]{1,0:T(8,128)S(1)}, f32[512,512]{1,0:T(8,128)S(1)}) custom-call(f32[512,512]{1,0:T(8,128)S(1)} %get-tuple-element.33.after_gain, f32[512,512]{1,0:T(8,128)S(1)} %get-tuple-element.34.after_noise, f32[512,512]{1,0:T(8,128)S(1)} %bitcast.5, ...), custom_call_target="tpu_custom_call" | custom-call | flops 6442450944 | bytes 11534336 | tf_op jit(solution)/shard_map/T_z/pallas_call | solution.py:68
  67.7 2.5 %collective-permute-done.10.mine = f32[136,512]{1,0:T(8,128)S(1)} collective-permute-done((f32[136,512]{1,0:T(8,128)S(1)}, f32[136,512]{1,0:T(8,128)S(1)}, u32[]{:S(2)}, u32[]{:S(2)}) %collective-permute-start.10) | collective-permute-done | bytes 278560 | tf_op jit(solution)/shard_map/T_z/ppermute | solution.py:27
  70.3 2.0 %collective-permute-start.11 = (f32[136,512]{1,0:T(8,128)S(1)}, f32[136,512]{1,0:T(8,128)S(1)}, u32[]{:S(2)}, u32[]{:S(2)}) collective-permute-start(f32[136,512]{1,0:T(8,128)S(1)} %collective-permute-done.10.mine), channel_id=1, source_target_pairs={{4,0},{0,4},{12,8},{8,12},{20,16},{16,20},{28,24},{24,28},{36,32},... | collective-permute-start | bytes 835592 | tf_op jit(solution)/shard_map/T_z/ppermute | solution.py:27
  72.2 1.2 collective-permute-done.11.other
  73.4 1.9 %T_z.4 = (f32[512,512]{1,0:T(8,128)S(1)}, f32[136,512]{1,0:T(8,128)S(1)}) custom-call(f32[136,512]{1,0:T(8,128)S(1)} %collective-permute-done.10.mine, f32[136,512]{1,0:T(8,128)S(1)} %collective-permute-done.11.other, f32[512,512]{1,0:T(8,128)S(1)} %get-tuple-element.40.gain, f32[512,512]{1,0:T(8,128)S(1)} %get-tuple-element.41.noise), custom_call_target="tpu_custom_call" | custom-call | flops 1610612736 | bytes 4194304 | tf_op jit(solution)/shard_map/T_z/pallas_call | solution.py:68
  75.3 1.3 collective-permute-start.14
  76.6 0.7 collective-permute-start.12
  77.3 4.2 %collective-permute-done.16.mine = f32[256,512]{1,0:T(8,128)S(1)} collective-permute-done((f32[256,512]{1,0:T(8,128)S(1)}, f32[256,512]{1,0:T(8,128)S(1)}, u32[]{:S(2)}, u32[]{:S(2)}) %collective-permute-start.16) | collective-permute-done | bytes 524320 | tf_op jit(solution)/shard_map/T_z/ppermute | solution.py:27
  81.5 1.2 collective-permute-start.17
  82.7 3.9 %collective-permute-done.14.far = f32[136,512]{1,0:T(8,128)S(1)} collective-permute-done((f32[136,512]{1,0:T(8,128)S(1)}, f32[136,512]{1,0:T(8,128)S(1)}, u32[]{:S(2)}, u32[]{:S(2)}) %collective-permute-start.14) | collective-permute-done | bytes 278560 | tf_op jit(solution)/shard_map/T_z/ppermute | solution.py:27
  86.6 1.2 collective-permute-start.15
  87.8 0.0 collective-permute-start.13
  87.8 1.2 collective-permute-done.15.far_other
  89.0 0.4 collective-permute-done.13.near_other
  89.4 6.0 %T_z.5 = (f32[512,512]{1,0:T(8,128)}, f32[256,512]{1,0:T(8,128)S(1)}, f32[256,512]{1,0:T(8,128)S(1)}) custom-call(f32[136,512]{1,0:T(8,128)S(1)} %collective-permute-done.12.near, f32[136,512]{1,0:T(8,128)S(1)} %collective-permute-done.13.near_other, f32[136,512]{1,0:T(8,128)S(1)} %collective-permute-done.14.far, ...), custom_call_target="tpu_custom_call" | custom-call | flops 4026531840 | bytes 10485760 | tf_op jit(solution)/shard_map/T_z/pallas_call | solution.py:68
  95.4 0.4 collective-permute-start.18
  95.7 1.5 %collective-permute-done.18.given = f32[256,512]{1,0:T(8,128)S(1)} collective-permute-done((f32[256,512]{1,0:T(8,128)S(1)}, f32[256,512]{1,0:T(8,128)S(1)}, u32[]{:S(2)}, u32[]{:S(2)}) %collective-permute-start.18) | collective-permute-done | bytes 524320 | tf_op jit(solution)/shard_map/T_reduce/ppermute | solution.py:27
  97.3 0.1 T_reduce.5
  97.4 0.1 collective-permute-start.19
  97.4 0.5 collective-permute-start.20
  98.0 2.1 %collective-permute-start.21 = (f32[64,512]{1,0:T(8,128)S(1)}, f32[64,512]{1,0:T(8,128)S(1)}, u32[]{:S(2)}, u32[]{:S(2)}) collective-permute-start(f32[64,512]{1,0:T(8,128)S(1)} %get-tuple-element.55), channel_id=1, source_target_pairs={{8,0},{12,4},{16,8},{20,12},{24,16},{28,20},{0,24},{4,28},{40,32},... | collective-permute-start | bytes 393224 | tf_op jit(solution)/shard_map/T_reduce/ppermute | solution.py:27
  100.1 6.2 %collective-permute-done.19.b = f32[64,512]{1,0:T(8,128)S(1)} collective-permute-done((f32[64,512]{1,0:T(8,128)S(1)}, f32[64,512]{1,0:T(8,128)S(1)}, u32[]{:S(2)}, u32[]{:S(2)}) %collective-permute-start.19) | collective-permute-done | bytes 131104 | tf_op jit(solution)/shard_map/T_reduce/ppermute | solution.py:27
  106.4 0.2 collective-permute-done.21.d
  106.5 0.1 collective-permute-start.24
  106.6 0.1 collective-permute-start.23
  106.7 2.6 %collective-permute-start.22 = (f32[64,512]{1,0:T(8,128)S(1)}, f32[64,512]{1,0:T(8,128)S(1)}, u32[]{:S(2)}, u32[]{:S(2)}) collective-permute-start(f32[64,512]{1,0:T(8,128)S(1)} %T_reduce.6.refs_0_), channel_id=1, source_target_pairs={{32,0},{36,4},{40,8},{44,12},{48,16},{52,20},{56,24},{60,28},{64,3... | collective-permute-start | bytes 393224 | tf_op jit(solution)/shard_map/T_reduce/ppermute | solution.py:27
  109.3 6.3 %collective-permute-done.24.refs_3_ = f32[64,512]{1,0:T(8,128)S(1)} collective-permute-done((f32[64,512]{1,0:T(8,128)S(1)}, f32[64,512]{1,0:T(8,128)S(1)}, u32[]{:S(2)}, u32[]{:S(2)}) %collective-permute-start.24) | collective-permute-done | bytes 131104 | tf_op jit(solution)/shard_map/T_reduce/ppermute | solution.py:27
  115.6 0.1 T_reduce.7.a
  115.7 0.7 collective-permute-start.27
  116.4 3.4 %collective-permute-start.26 = (f32[64,512]{1,0:T(8,128)S(1)}, f32[64,512]{1,0:T(8,128)S(1)}, u32[]{:S(2)}, u32[]{:S(2)}) collective-permute-start(f32[64,512]{1,0:T(8,128)S(1)} %T_reduce.7.a), channel_id=1, source_target_pairs={{16,0},{20,4},{24,8},{28,12},{0,16},{4,20},{8,24},{12,28},{48,32},... | collective-permute-start | bytes 393224 | tf_op jit(solution)/shard_map/T_reduce/ppermute | solution.py:27
  119.7 1.2 collective-permute-done.27.d
  120.9 3.3 %collective-permute-done.26.c = f32[64,512]{1,0:T(8,128)S(1)} collective-permute-done((f32[64,512]{1,0:T(8,128)S(1)}, f32[64,512]{1,0:T(8,128)S(1)}, u32[]{:S(2)}, u32[]{:S(2)}) %collective-permute-start.26) | collective-permute-done | bytes 131104 | tf_op jit(solution)/shard_map/T_reduce/ppermute | solution.py:27
  124.2 0.6 collective-permute-done.25.b
  124.8 0.1 T_reduce.8.mine
  124.9 2.3 %collective-permute-start.28 = (f32[256,512]{1,0:T(8,128)S(1)}, f32[256,512]{1,0:T(8,128)S(1)}, u32[]{:S(2)}, u32[]{:S(2)}) collective-permute-start(f32[256,512]{1,0:T(8,128)S(1)} %T_reduce.8.mine), channel_id=1, source_target_pairs={{4,0},{0,4},{12,8},{8,12},{20,16},{16,20},{28,24},{24,28},{36,32},... | collective-permute-start | bytes 1572872 | tf_op jit(solution)/shard_map/T_reduce/ppermute | solution.py:27
  127.2 1.5 %collective-permute-done.28.other = f32[256,512]{1,0:T(8,128)S(1)} collective-permute-done((f32[256,512]{1,0:T(8,128)S(1)}, f32[256,512]{1,0:T(8,128)S(1)}, u32[]{:S(2)}, u32[]{:S(2)}) %collective-permute-start.28) | collective-permute-done | bytes 524320 | tf_op jit(solution)/shard_map/T_reduce/ppermute | solution.py:27
  128.7 1.1 T_reduce.9
  (16 shorter events, 0.1 us)
Async XLA Ops:
  0.6 4.0 %collective-permute-start = (f32[512,512]{1,0:T(8,128)}, f32[512,512]{1,0:T(8,128)S(1)}, u32[]{:S(2)}, u32[]{:S(2)}) collective-permute-start(f32[512,512]{1,0:T(8,128)} %bitcast.3), channel_id=1, source_target_pairs={{4,0},{0,4},{12,8},{8,12},{20,16},{16,20},{28,24},{24,28},{36,32},... | collective-permute-start | bytes 3145736 | tf_op jit(solution)/shard_map/T_chip/ppermute | solution.py:27
  2.1 4.0 %collective-permute-start.1 = (f32[512,512]{1,0:T(8,128)}, f32[512,512]{1,0:T(8,128)S(1)}, u32[]{:S(2)}, u32[]{:S(2)}) collective-permute-start(f32[512,512]{1,0:T(8,128)} %bitcast.6), channel_id=1, source_target_pairs={{4,0},{0,4},{12,8},{8,12},{20,16},{16,20},{28,24},{24,28},{36,32},... | collective-permute-start | bytes 3145736 | tf_op jit(solution)/shard_map/T_chip/ppermute | solution.py:27
  6.1 1.2 copy-start
  7.4 1.2 copy-start.2
  12.0 19.8 %collective-permute-start.2 = (f32[392,512]{1,0:T(8,128)S(1)}, f32[392,512]{1,0:T(8,128)S(1)}, u32[]{:S(2)}, u32[]{:S(2)}) collective-permute-start(f32[392,512]{1,0:T(8,128)S(1)} %get-tuple-element.31), channel_id=1, source_target_pairs={{8,0},{12,4},{16,8},{20,12},{24,16},{28,20},{0,24},{4,28},{40,32},... | collective-permute-start | bytes 2408456 | tf_op jit(solution)/shard_map/T_row/ppermute | solution.py:27
  14.9 20.4 %collective-permute-start.4 = (f32[392,512]{1,0:T(8,128)S(1)}, f32[392,512]{1,0:T(8,128)S(1)}, u32[]{:S(2)}, u32[]{:S(2)}) collective-permute-start(f32[392,512]{1,0:T(8,128)S(1)} %get-tuple-element.31), channel_id=1, source_target_pairs={{24,0},{28,4},{0,8},{4,12},{8,16},{12,20},{16,24},{20,28},{56,32},... | collective-permute-start | bytes 2408456 | tf_op jit(solution)/shard_map/T_row/ppermute | solution.py:27
  31.8 11.0 %collective-permute-start.6 = (f32[200,512]{1,0:T(8,128)S(1)}, f32[200,512]{1,0:T(8,128)S(1)}, u32[]{:S(2)}, u32[]{:S(2)}) collective-permute-start(f32[200,512]{1,0:T(8,128)S(1)} %slice.8), channel_id=1, source_target_pairs={{8,0},{12,4},{16,8},{20,12},{24,16},{28,20},{0,24},{4,28},{40,32},... | collective-permute-start | bytes 1228808 | tf_op jit(solution)/shard_map/T_row/ppermute | solution.py:27
  35.3 15.7 %collective-permute-start.5 = (f32[392,512]{1,0:T(8,128)S(1)}, f32[392,512]{1,0:T(8,128)S(1)}, u32[]{:S(2)}, u32[]{:S(2)}) collective-permute-start(f32[392,512]{1,0:T(8,128)S(1)} %collective-permute-done.4.refs_2_), channel_id=1, source_target_pairs={{4,0},{0,4},{12,8},{8,12},{20,16},{16,20},{28,24},{24,28},{36,32},... | collective-permute-start | bytes 2408456 | tf_op jit(solution)/shard_map/T_row/ppermute | solution.py:27
  36.8 14.2 %collective-permute-start.3 = (f32[392,512]{1,0:T(8,128)S(1)}, f32[392,512]{1,0:T(8,128)S(1)}, u32[]{:S(2)}, u32[]{:S(2)}) collective-permute-start(f32[392,512]{1,0:T(8,128)S(1)} %collective-permute-done.2.refs_0_), channel_id=1, source_target_pairs={{4,0},{0,4},{12,8},{8,12},{20,16},{16,20},{28,24},{24,28},{36,32},... | collective-permute-start | bytes 2408456 | tf_op jit(solution)/shard_map/T_row/ppermute | solution.py:27
  36.8 11.4 %collective-permute-start.8 = (f32[192,512]{1,0:T(8,128)S(1)}, f32[192,512]{1,0:T(8,128)S(1)}, u32[]{:S(2)}, u32[]{:S(2)}) collective-permute-start(f32[192,512]{1,0:T(8,128)S(1)} %slice.9), channel_id=1, source_target_pairs={{24,0},{28,4},{0,8},{4,12},{8,16},{12,20},{16,24},{20,28},{56,32},... | collective-permute-start | bytes 1179656 | tf_op jit(solution)/shard_map/T_row/ppermute | solution.py:27
  42.8 8.1 %collective-permute-start.7 = (f32[200,512]{1,0:T(8,128)S(1)}, f32[200,512]{1,0:T(8,128)S(1)}, u32[]{:S(2)}, u32[]{:S(2)}) collective-permute-start(f32[200,512]{1,0:T(8,128)S(1)} %collective-permute-done.6.refs_4_), channel_id=1, source_target_pairs={{4,0},{0,4},{12,8},{8,12},{20,16},{16,20},{28,24},{24,28},{36,32},... | collective-permute-start | bytes 1228808 | tf_op jit(solution)/shard_map/T_row/ppermute | solution.py:27
  48.2 2.7 %collective-permute-start.9 = (f32[192,512]{1,0:T(8,128)S(1)}, f32[192,512]{1,0:T(8,128)S(1)}, u32[]{:S(2)}, u32[]{:S(2)}) collective-permute-start(f32[192,512]{1,0:T(8,128)S(1)} %collective-permute-done.8.refs_6_), channel_id=1, source_target_pairs={{4,0},{0,4},{12,8},{8,12},{20,16},{16,20},{28,24},{24,28},{36,32},... | collective-permute-start | bytes 1179656 | tf_op jit(solution)/shard_map/T_row/ppermute | solution.py:27
  51.0 12.1 %copy-start.1 = (f32[1,512,512]{2,1,0:T(8,128)S(1)}, f32[1,512,512]{2,1,0:T(8,128)}, u32[]{:S(2)}) copy-start(f32[1,512,512]{2,1,0:T(8,128)} %param.3) | copy-start | bytes 3145732
  51.0 12.1 %copy-start.3 = (f32[1,512,512]{2,1,0:T(8,128)S(1)}, f32[1,512,512]{2,1,0:T(8,128)}, u32[]{:S(2)}) copy-start(f32[1,512,512]{2,1,0:T(8,128)} %param.4) | copy-start | bytes 3145732
  51.0 12.1 %copy-start.4 = (f32[512,512]{1,0:T(8,128)S(1)}, f32[512,512]{1,0:T(8,128)}, u32[]{:S(2)}) copy-start(f32[512,512]{1,0:T(8,128)} %estimate.1) | copy-start | bytes 3145732
  60.5 9.8 %collective-permute-start.10 = (f32[136,512]{1,0:T(8,128)S(1)}, f32[136,512]{1,0:T(8,128)S(1)}, u32[]{:S(2)}, u32[]{:S(2)}) collective-permute-start(f32[136,512]{1,0:T(8,128)S(1)} %get-tuple-element.32), channel_id=1, source_target_pairs={{32,0},{36,4},{40,8},{44,12},{48,16},{52,20},{56,24},{60,28},{96,6... | collective-permute-start | bytes 835592 | tf_op jit(solution)/shard_map/T_z/ppermute | solution.py:27
  61.8 19.7 %collective-permute-start.16 = (f32[256,512]{1,0:T(8,128)S(1)}, f32[256,512]{1,0:T(8,128)S(1)}, u32[]{:S(2)}, u32[]{:S(2)}) collective-permute-start(f32[256,512]{1,0:T(8,128)S(1)} %get-tuple-element.43), channel_id=1, source_target_pairs={{32,0},{36,4},{40,8},{44,12},{48,16},{52,20},{56,24},{60,28},{33,1... | collective-permute-start | bytes 1572872 | tf_op jit(solution)/shard_map/T_z/ppermute | solution.py:27
  70.3 3.1 %collective-permute-start.11 = (f32[136,512]{1,0:T(8,128)S(1)}, f32[136,512]{1,0:T(8,128)S(1)}, u32[]{:S(2)}, u32[]{:S(2)}) collective-permute-start(f32[136,512]{1,0:T(8,128)S(1)} %collective-permute-done.10.mine), channel_id=1, source_target_pairs={{4,0},{0,4},{12,8},{8,12},{20,16},{16,20},{28,24},{24,28},{36,32},... | collective-permute-start | bytes 835592 | tf_op jit(solution)/shard_map/T_z/ppermute | solution.py:27
  75.3 11.3 %collective-permute-start.14 = (f32[136,512]{1,0:T(8,128)S(1)}, f32[136,512]{1,0:T(8,128)S(1)}, u32[]{:S(2)}, u32[]{:S(2)}) collective-permute-start(f32[136,512]{1,0:T(8,128)S(1)} %get-tuple-element.42), channel_id=1, source_target_pairs={{64,0},{68,4},{72,8},{76,12},{80,16},{84,20},{88,24},{92,28},{65,1... | collective-permute-start | bytes 835592 | tf_op jit(solution)/shard_map/T_z/ppermute | solution.py:27
  76.6 11.2 %collective-permute-start.12 = (f32[136,512]{1,0:T(8,128)S(1)}, f32[136,512]{1,0:T(8,128)S(1)}, u32[]{:S(2)}, u32[]{:S(2)}) collective-permute-start(f32[136,512]{1,0:T(8,128)S(1)} %get-tuple-element.42), channel_id=1, source_target_pairs={{64,32},{68,36},{72,40},{76,44},{80,48},{84,52},{88,56},{92,60},{6... | collective-permute-start | bytes 835592 | tf_op jit(solution)/shard_map/T_z/ppermute | solution.py:27
  81.5 6.3 %collective-permute-start.17 = (f32[256,512]{1,0:T(8,128)S(1)}, f32[256,512]{1,0:T(8,128)S(1)}, u32[]{:S(2)}, u32[]{:S(2)}) collective-permute-start(f32[256,512]{1,0:T(8,128)S(1)} %collective-permute-done.16.mine), channel_id=1, source_target_pairs={{4,0},{0,4},{12,8},{8,12},{20,16},{16,20},{28,24},{24,28},{36,32},... | collective-permute-start | bytes 1572872 | tf_op jit(solution)/shard_map/T_z/ppermute | solution.py:27
  86.6 2.4 %collective-permute-start.15 = (f32[136,512]{1,0:T(8,128)S(1)}, f32[136,512]{1,0:T(8,128)S(1)}, u32[]{:S(2)}, u32[]{:S(2)}) collective-permute-start(f32[136,512]{1,0:T(8,128)S(1)} %collective-permute-done.14.far), channel_id=1, source_target_pairs={{4,0},{0,4},{12,8},{8,12},{20,16},{16,20},{28,24},{24,28},{36,32},... | collective-permute-start | bytes 835592 | tf_op jit(solution)/shard_map/T_z/ppermute | solution.py:27
  87.8 1.6 %collective-permute-start.13 = (f32[136,512]{1,0:T(8,128)S(1)}, f32[136,512]{1,0:T(8,128)S(1)}, u32[]{:S(2)}, u32[]{:S(2)}) collective-permute-start(f32[136,512]{1,0:T(8,128)S(1)} %collective-permute-done.12.near), channel_id=1, source_target_pairs={{4,0},{0,4},{12,8},{8,12},{20,16},{16,20},{28,24},{24,28},{36,32},... | collective-permute-start | bytes 835592 | tf_op jit(solution)/shard_map/T_z/ppermute | solution.py:27
  95.4 1.9 %collective-permute-start.18 = (f32[256,512]{1,0:T(8,128)S(1)}, f32[256,512]{1,0:T(8,128)S(1)}, u32[]{:S(2)}, u32[]{:S(2)}) collective-permute-start(f32[256,512]{1,0:T(8,128)S(1)} %get-tuple-element.51), channel_id=1, source_target_pairs={{4,0},{0,4},{12,8},{8,12},{20,16},{16,20},{28,24},{24,28},{36,32},... | collective-permute-start | bytes 1572872 | tf_op jit(solution)/shard_map/T_reduce/ppermute | solution.py:27
  97.4 9.0 %collective-permute-start.19 = (f32[64,512]{1,0:T(8,128)S(1)}, f32[64,512]{1,0:T(8,128)S(1)}, u32[]{:S(2)}, u32[]{:S(2)}) collective-permute-start(f32[64,512]{1,0:T(8,128)S(1)} %get-tuple-element.53), channel_id=1, source_target_pairs={{24,0},{28,4},{0,8},{4,12},{8,16},{12,20},{16,24},{20,28},{56,32},... | collective-permute-start | bytes 393224 | tf_op jit(solution)/shard_map/T_reduce/ppermute | solution.py:27
  97.4 8.9 %collective-permute-start.20 = (f32[64,512]{1,0:T(8,128)S(1)}, f32[64,512]{1,0:T(8,128)S(1)}, u32[]{:S(2)}, u32[]{:S(2)}) collective-permute-start(f32[64,512]{1,0:T(8,128)S(1)} %get-tuple-element.54), channel_id=1, source_target_pairs={{16,0},{20,4},{24,8},{28,12},{0,16},{4,20},{8,24},{12,28},{48,32},... | collective-permute-start | bytes 393224 | tf_op jit(solution)/shard_map/T_reduce/ppermute | solution.py:27
  98.0 8.5 %collective-permute-start.21 = (f32[64,512]{1,0:T(8,128)S(1)}, f32[64,512]{1,0:T(8,128)S(1)}, u32[]{:S(2)}, u32[]{:S(2)}) collective-permute-start(f32[64,512]{1,0:T(8,128)S(1)} %get-tuple-element.55), channel_id=1, source_target_pairs={{8,0},{12,4},{16,8},{20,12},{24,16},{28,20},{0,24},{4,28},{40,32},... | collective-permute-start | bytes 393224 | tf_op jit(solution)/shard_map/T_reduce/ppermute | solution.py:27
  106.5 9.0 %collective-permute-start.24 = (f32[64,512]{1,0:T(8,128)S(1)}, f32[64,512]{1,0:T(8,128)S(1)}, u32[]{:S(2)}, u32[]{:S(2)}) collective-permute-start(f32[64,512]{1,0:T(8,128)S(1)} %T_reduce.6.refs_0_), channel_id=1, source_target_pairs={{96,0},{100,4},{104,8},{108,12},{112,16},{116,20},{120,24},{124,28... | collective-permute-start | bytes 393224 | tf_op jit(solution)/shard_map/T_reduce/ppermute | solution.py:27
  106.6 8.9 %collective-permute-start.23 = (f32[64,512]{1,0:T(8,128)S(1)}, f32[64,512]{1,0:T(8,128)S(1)}, u32[]{:S(2)}, u32[]{:S(2)}) collective-permute-start(f32[64,512]{1,0:T(8,128)S(1)} %T_reduce.6.refs_0_), channel_id=1, source_target_pairs={{64,0},{68,4},{72,8},{76,12},{80,16},{84,20},{88,24},{92,28},{96,3... | collective-permute-start | bytes 393224 | tf_op jit(solution)/shard_map/T_reduce/ppermute | solution.py:27
  106.7 8.8 %collective-permute-start.22 = (f32[64,512]{1,0:T(8,128)S(1)}, f32[64,512]{1,0:T(8,128)S(1)}, u32[]{:S(2)}, u32[]{:S(2)}) collective-permute-start(f32[64,512]{1,0:T(8,128)S(1)} %T_reduce.6.refs_0_), channel_id=1, source_target_pairs={{32,0},{36,4},{40,8},{44,12},{48,16},{52,20},{56,24},{60,28},{64,3... | collective-permute-start | bytes 393224 | tf_op jit(solution)/shard_map/T_reduce/ppermute | solution.py:27
  115.7 5.2 %collective-permute-start.27 = (f32[64,512]{1,0:T(8,128)S(1)}, f32[64,512]{1,0:T(8,128)S(1)}, u32[]{:S(2)}, u32[]{:S(2)}) collective-permute-start(f32[64,512]{1,0:T(8,128)S(1)} %T_reduce.7.a), channel_id=1, source_target_pairs={{24,0},{28,4},{0,8},{4,12},{8,16},{12,20},{16,24},{20,28},{56,32},... | collective-permute-start | bytes 393224 | tf_op jit(solution)/shard_map/T_reduce/ppermute | solution.py:27
  116.4 7.9 %collective-permute-start.26 = (f32[64,512]{1,0:T(8,128)S(1)}, f32[64,512]{1,0:T(8,128)S(1)}, u32[]{:S(2)}, u32[]{:S(2)}) collective-permute-start(f32[64,512]{1,0:T(8,128)S(1)} %T_reduce.7.a), channel_id=1, source_target_pairs={{16,0},{20,4},{24,8},{28,12},{0,16},{4,20},{8,24},{12,28},{48,32},... | collective-permute-start | bytes 393224 | tf_op jit(solution)/shard_map/T_reduce/ppermute | solution.py:27
  119.7 5.1 %collective-permute-start.25 = (f32[64,512]{1,0:T(8,128)S(1)}, f32[64,512]{1,0:T(8,128)S(1)}, u32[]{:S(2)}, u32[]{:S(2)}) collective-permute-start(f32[64,512]{1,0:T(8,128)S(1)} %T_reduce.7.a), channel_id=1, source_target_pairs={{8,0},{12,4},{16,8},{20,12},{24,16},{28,20},{0,24},{4,28},{40,32},... | collective-permute-start | bytes 393224 | tf_op jit(solution)/shard_map/T_reduce/ppermute | solution.py:27
  124.9 3.9 %collective-permute-start.28 = (f32[256,512]{1,0:T(8,128)S(1)}, f32[256,512]{1,0:T(8,128)S(1)}, u32[]{:S(2)}, u32[]{:S(2)}) collective-permute-start(f32[256,512]{1,0:T(8,128)S(1)} %T_reduce.8.mine), channel_id=1, source_target_pairs={{4,0},{0,4},{12,8},{8,12},{20,16},{16,20},{28,24},{24,28},{36,32},... | collective-permute-start | bytes 1572872 | tf_op jit(solution)/shard_map/T_reduce/ppermute | solution.py:27

commit v2 on v1

v2 whole, which is shorter than its diff:
```python
import jax
import jax.numpy as jnp
from jax import lax
from jax.experimental import pallas as pl
from jax.experimental.pallas import tpu as pltpu
from jax.sharding import PartitionSpec as P

ROWS = 4
CHIPS = 4
CORES = 2
PAD = 8
VMEM_LIMIT = 24 * 2**20


def device(z, y, core):
    return ((z % ROWS) * CHIPS + y % CHIPS) * CORES + core


def moved(x, source):
    pairs = []
    for z in range(ROWS):
        for y in range(CHIPS):
            for c in range(CORES):
                origin = source(z, y, c)
                if origin is not None:
                    pairs.append((device(*origin), device(z, y, c)))
    return lax.ppermute(x, "tm", pairs)


def swap_cores(x):
    return moved(x, lambda z, y, c: (z, y, 1 - c))


def from_chip_ahead(x, distance):
    return moved(x, lambda z, y, c: (z, y + distance, c))


def from_row_ahead(x, distance, rows=tuple(range(ROWS))):
    return moved(x, lambda z, y, c: (z + distance, y, c) if z in rows else None)


def place():
    here = lax.axis_index("tm")
    return here // (CHIPS * CORES), (here // CORES) % CHIPS, here % CORES


def split(x):
    high = x.astype(jnp.bfloat16)
    return high, (x - high.astype(jnp.float32)).astype(jnp.bfloat16)


def dot3(left, right, contract=0):
    def one(a, b):
        return lax.dot_general(
            a, b, (((1,), (contract,)), ((), ())), preferred_element_type=jnp.float32
        )

    (left_high, left_low), (right_high, right_low) = left, right
    return one(left_low, right_high) + one(left_high, right_low) + one(left_high, right_high)


def carry(gain, cov, noise):
    return noise + dot3(split(dot3(gain, split(cov))), gain, 1)


def kernel_call(body, shapes, operands, scratch=(), flops=0, moved_bytes=0, in_hbm=0):
    vmem, hbm = pl.BlockSpec(memory_space=pltpu.VMEM), pl.BlockSpec(memory_space=pltpu.HBM)
    semaphores = [pltpu.SemaphoreType.DMA((in_hbm,))] if in_hbm else []
    return pl.pallas_call(
        body,
        out_shape=[
            jax.ShapeDtypeStruct(shape, jnp.float32) if type(shape) is tuple else shape for shape in shapes
        ],
        in_specs=[hbm] * in_hbm + [vmem] * (len(operands) - in_hbm),
        out_specs=[vmem] * len(shapes),
        scratch_shapes=[pltpu.VMEM(shape, jnp.float32) for shape in scratch] + semaphores,
        compiler_params=pltpu.CompilerParams(vmem_limit_bytes=VMEM_LIMIT),
        cost_estimate=pl.CostEstimate(flops=flops, bytes_accessed=moved_bytes, transcendentals=0),
    )(*operands)


def rows_at(index, size):
    return pl.ds(pl.multiple_of(index * size, size), size)


def triangles(half):
    rows = lax.broadcasted_iota(jnp.int32, (half, half), 0)
    columns = lax.broadcasted_iota(jnp.int32, (half, half), 1)
    return rows >= columns, rows == columns


def pack(x, out_ref, start, core):
    half = x.shape[0] // 2
    quarter = half // 2
    lower, on_diagonal = triangles(half)
    a, b, d = x[:half, :half], x[:half, half:], x[half:, half:]
    diagonal = jnp.sum(jnp.where(on_diagonal, d, 0.0), axis=0, keepdims=True)
    w = jnp.where(core == 0, jnp.where(lower, a, d), b)
    out_ref[start : start + quarter, :half] = w[:quarter]
    out_ref[start : start + quarter, half:] = w[quarter:]
    out_ref[start + quarter : start + quarter + PAD, :half] = jnp.broadcast_to(diagonal, (PAD, half))
    out_ref[start + quarter : start + quarter + PAD, half:] = jnp.broadcast_to(diagonal, (PAD, half))


def unpack(mine, other, core):
    half = mine.shape[1] // 2
    quarter = half // 2
    lower, on_diagonal = triangles(half)

    def square(x):
        return jnp.concatenate([x[:quarter, :half], x[:quarter, half:]], axis=0)

    diagonal = jnp.where(core == 0, mine, other)[quarter : quarter + 1, :half]
    mine, other = square(mine), square(other)
    w = jnp.where(core == 0, mine, other)
    b = jnp.where(core == 0, other, mine)
    flipped = w.T
    a = jnp.where(lower, w, flipped)
    d = jnp.where(on_diagonal, diagonal, jnp.where(lower, flipped, w))
    top = jnp.concatenate([a, b], axis=1)
    return jnp.concatenate([top, jnp.concatenate([b.T, d], axis=1)], axis=0)


def chip_gain_kernel(gain, gain_other, gain_ref, send_ref, g_ref, sems):
    _, _, core = place()
    copy = pltpu.make_async_copy(gain, g_ref.at[core], sems.at[0])
    copy.start()
    g_ref[1 - core] = gain_other[...]
    copy.wait()
    gain_ref[...] = dot3(split(g_ref[0]), split(g_ref[1]))
    send_ref[...] = gain_ref[rows_at(core, send_ref.shape[0]), :]


def chip_noise_kernel(gain, noise, gain_other, noise_other, noise_ref, packed_ref, g_ref, n_ref, sems):
    _, _, core = place()
    copies = [
        pltpu.make_async_copy(gain, g_ref.at[core], sems.at[0]),
        pltpu.make_async_copy(noise, n_ref.at[core], sems.at[1]),
    ]
    for copy in copies:
        copy.start()
    g_ref[1 - core], n_ref[1 - core] = gain_other[...], noise_other[...]
    for copy in copies:
        copy.wait()
    result = carry(split(g_ref[0]), n_ref[1], n_ref[0])
    noise_ref[...] = result
    pack(result, packed_ref, 0, core)


def row_gains_kernel(own, *refs):
    ahead, ahead_other, behind, behind_other, far, far_other, rest, rest_other = refs[:8]
    high_ref, low_ref, after_ref, row_ref, mine_ref, p_ref = refs[8:]
    _, y, core = place()
    width = own.shape[0]
    half = width // 2
    p_ref[y] = own[...]
    for slot, mine, other in (
        ((y + 1) % CHIPS, ahead, ahead_other),
        ((y + 3) % CHIPS, behind, behind_other),
    ):
        p_ref[slot, rows_at(core, half), :] = mine[...]
        p_ref[slot, rows_at(1 - core, half), :] = other[...]
    slot = (y + 2) % CHIPS
    cut = half // 2
    for place_of, upper, lower in ((core, far, rest), (1 - core, far_other, rest_other)):
        p_ref[slot, rows_at(2 * place_of, cut), :] = upper[:cut]
        p_ref[slot, rows_at(2 * place_of + 1, cut), :] = lower[:cut]

    gain = p_ref[CHIPS - 1]

    @pl.when(y == CHIPS - 1)
    def _():
        rows = lax.broadcasted_iota(jnp.int32, (width, width), 0)
        columns = lax.broadcasted_iota(jnp.int32, (width, width), 1)
        after_ref[...] = jnp.where(rows == columns, 1.0, 0.0)

    for k in range(CHIPS - 2, -1, -1):
        @pl.when(y == k)
        def _(gain=gain):
            after_ref[...] = gain

        step = split(p_ref[k])
        high_ref[k], low_ref[k] = step
        gain = dot3(step, split(gain))
    row_ref[...] = gain
    mine_ref[...] = row_ref[rows_at(core, half), :]


def row_noises_kernel(high_ref, low_ref, own, *refs):
    ahead, ahead_other, behind, behind_other, far, far_other, rest, rest_other = refs[:8]
    after_ref, noise_ref, packed_ref, n_ref = refs[8:]
    _, y, core = place()
    n_ref[y] = own[...]
    n_ref[(y + 1) % CHIPS] = unpack(ahead[...], ahead_other[...], core)
    n_ref[(y + 3) % CHIPS] = unpack(behind[...], behind_other[...], core)
    cut = own.shape[0] // 4
    n_ref[(y + 2) % CHIPS] = unpack(
        jnp.concatenate([far[cut:], rest[cut:]], axis=0),
        jnp.concatenate([far_other[cut:], rest_other[cut:]], axis=0),
        core,
    )
    noise = n_ref[CHIPS - 1]

    @pl.when(y == CHIPS - 1)
    def _():
        after_ref[...] = jnp.zeros_like(after_ref)

    for k in range(CHIPS - 2, -1, -1):
        @pl.when(y == k)
        def _(noise=noise):
            after_ref[...] = noise

        noise = carry((high_ref[k], low_ref[k]), noise, n_ref[k])
    noise_ref[...] = noise
    pack(noise, packed_ref, 0, core)


def after_kernel(
    after_gain, after_noise, gain, gain_other, noise, noise_other, estimate,
    from_gain_ref, from_noise_ref, grad_gain_ref, grad_noise_ref, g_ref, n_ref,
):
    _, _, core = place()

    @pl.when(core == 0)
    def _():
        other = split(gain_other[...])
        g_ref[...] = dot3(other, split(after_gain[...]))
        n_ref[...] = carry(other, after_noise[...], noise_other[...])

    @pl.when(core != 0)
    def _():
        g_ref[...] = after_gain[...]
        n_ref[...] = after_noise[...]

    own, transition = split(gain[...]), split(estimate[...])
    from_gain = dot3(own, split(g_ref[...]))
    from_gain_ref[...] = from_gain
    grad_gain_ref[...] = g_ref[...] - dot3(transition, split(from_gain))
    lagged = dot3(split(n_ref[...]), own, 1)
    from_noise = dot3(own, split(lagged)) + noise[...]
    from_noise_ref[...] = from_noise
    grad_noise_ref[...] = lagged - dot3(transition, split(from_noise))


def next_row_kernel(mine, other, gain, noise, next_ref, packed_ref):
    _, _, core = place()
    following = unpack(mine[...], other[...], core)
    next_ref[...] = following
    pack(carry(split(gain[...]), following, noise[...]), packed_ref, 0, core)


def final_kernel(
    near, near_other, far, far_other, lead, lead_other, first, first_other, following, from_gain, grad_gain, grad_noise,
    carried_ref, keep_ref, give_ref, t_ref, g_ref,
):
    z, y, core = place()
    half = keep_ref.shape[0]

    @pl.when(z == 0)
    def _():
        g_ref[rows_at(core, half), :] = lead[...]
        g_ref[rows_at(1 - core, half), :] = lead_other[...]
        second = unpack(far[...], far_other[...], core)
        t_ref[...] = carry(split(g_ref[...]), second, unpack(first[...], first_other[...], core))

    @pl.when(z == 1)
    def _():
        t_ref[...] = unpack(near[...], near_other[...], core)

    @pl.when(z == 2)
    def _():
        t_ref[...] = following[...]

    @pl.when(z == 3)
    def _():
        t_ref[...] = jnp.zeros_like(t_ref)

    gain = split(from_gain[...])
    carried_ref[...] = dot3(split(t_ref[...]), gain, 1)
    carried = split(carried_ref[...])
    last = (z == ROWS - 1) & (y == CHIPS - 1) & (core == CORES - 1)
    terms = jnp.where(last, 0.0, grad_noise[...] + dot3(split(grad_gain[...]), carried))

    @pl.when(core == 0)
    def _():
        keep_ref[...], give_ref[...] = terms[:half], terms[half:]

    @pl.when(core != 0)
    def _():
        keep_ref[...], give_ref[...] = terms[half:], terms[:half]


def covariance_kernel(from_gain, from_noise, carried, out_ref):
    out_ref[...] = from_noise[...] + dot3(split(from_gain[...]), split(carried[...]))


def share_kernel(keep, given, out_ref):
    out_ref[...] = (keep[...] + given[...]).reshape(out_ref.shape)


def sum_kernel(count, pieces, out_ref):
    total = pieces[0]
    for k in range(1, pieces.shape[0]):
        total = total + pieces[k]
    total = total / count
    for k in range(pieces.shape[0]):
        out_ref[k] = total


def whole_kernel(mine, other, out_ref):
    _, _, core = place()
    half = mine.shape[0]
    out_ref[rows_at(core, half), :] = mine[...]
    out_ref[rows_at(1 - core, half), :] = other[...]


def on_device(transitions, cond_covs, transition_est):
    gain, noise = transitions[0], cond_covs[0]
    width = gain.shape[0]
    half = width // 2
    square, strip, piece = (width, width), (half, width), (half // 2 + PAD, width)
    groups = [[device(z, y, c) for z in range(ROWS) for y in range(CHIPS)] for c in range(CORES)]
    spread = (ROWS * CHIPS, half // (ROWS * CHIPS), width)
    flops = 6 * width**3
    size = 4 * width * width

    three = jax.ShapeDtypeStruct((CHIPS - 1, *square), jnp.bfloat16)

    with jax.named_scope("T_chip"):
        gain_other, noise_other = swap_cores(gain), swap_cores(noise)
        chip_gain, gain_mine = kernel_call(
            chip_gain_kernel, [square, strip], (gain, gain_other), [(CORES, *square)], flops, 4 * size, 1
        )
        chip_noise, noise_mine = kernel_call(
            chip_noise_kernel,
            [square, piece],
            (gain, noise, gain_other, noise_other),
            [(CORES, *square)] * 2,
            2 * flops,
            6 * size,
            2,
        )

    with jax.named_scope("T_row"):
        gains = [from_chip_ahead(gain_mine, r) for r in (1, 3)]
        noises = [from_chip_ahead(noise_mine, r) for r in (1, 3)]
        cut, cut_noise = half // 2, (piece[0] // 2 + PAD - 1) // PAD * PAD
        far = from_chip_ahead(jnp.concatenate([gains[0][:cut], noises[0][:cut_noise]], axis=0), 1)
        rest = from_chip_ahead(jnp.concatenate([gains[1][cut:], noises[1][cut_noise:]], axis=0), 3)
        gain_pieces, noise_pieces = [], []
        for x in (*gains, far, rest):
            gain_pieces += [x, swap_cores(x)]
        for x in noises:
            noise_pieces += [x, swap_cores(x)]
        high, low, after_gain, row_gain, row_gain_mine = kernel_call(
            row_gains_kernel,
            [three, three, square, square, strip],
            (chip_gain, *gain_pieces),
            [(CHIPS, *square)],
            3 * flops,
            10 * size,
        )
        after_noise, row_noise, row_packed = kernel_call(
            row_noises_kernel,
            [square, square, piece],
            (high, low, chip_noise, *noise_pieces, *gain_pieces[4:]),
            [(CHIPS, *square)],
            6 * flops,
            8 * size,
        )

    with jax.named_scope("T_z"):
        next_mine = from_row_ahead(row_packed, 1, (2,))
        leads = [from_row_ahead(x, 1, (0,)) for x in (row_gain_mine, row_packed)]
        parts = kernel_call(
            after_kernel,
            [square] * 4,
            (after_gain, after_noise, gain, gain_other, noise, noise_other, transition_est),
            [square] * 2,
            8 * flops,
            11 * size,
        )
        next_mine, *parts = lax.optimization_barrier((next_mine, *parts))
        from_gain, from_noise, grad_gain, grad_noise = parts
        next_noise, second_packed = kernel_call(
            next_row_kernel,
            [square, piece],
            (next_mine, swap_cores(next_mine), row_gain, row_noise),
            (),
            2 * flops,
            4 * size,
        )
        near, far = from_row_ahead(second_packed, 1, (1,)), from_row_ahead(second_packed, 2, (0,))
        carried, keep, give = kernel_call(
            final_kernel,
            [square, strip, strip],
            (
                near, swap_cores(near), far, swap_cores(far), leads[0], swap_cores(leads[0]), leads[1], swap_cores(leads[1]), next_noise,
                from_gain, grad_gain, grad_noise,
            ),
            [square] * 2,
            4 * flops,
            10 * size,
        )

        (covariance,) = kernel_call(
            covariance_kernel, [square], (from_gain, from_noise, carried), (), flops, 4 * size
        )

    with jax.named_scope("T_reduce"):
        (pieces,) = kernel_call(share_kernel, [spread], (keep, swap_cores(give)), (), size // 4, size)
        pieces = lax.all_to_all(pieces, "tm", 0, 0, axis_index_groups=groups)
        terms = lax.axis_size("tm") - 1
        (pieces,) = kernel_call(
            lambda *refs: sum_kernel(terms, *refs), [spread], (pieces,), (), size // 4, size
        )
        pieces = lax.all_to_all(pieces, "tm", 0, 0, axis_index_groups=groups)
        gradient_mine = pieces.reshape(strip)
        (gradient,) = kernel_call(
            whole_kernel, [square], (gradient_mine, swap_cores(gradient_mine)), (), size // 4, 2 * size
        )
    return covariance[None], gradient


def solution(mesh):
    return jax.shard_map(
        on_device,
        mesh=mesh,
        in_specs=(P(("rep", "tm"), None, None), P(("rep", "tm"), None, None), P("rep", None)),
        out_specs=(P(("rep", "tm"), None, None), P("rep", None)),
        check_vma=False,
    )
```

time: 130 us -> 122 us (0.938)
  waiting for transfers between devices: 65.6 us -> 35.8 us
  blocking collectives: 0 us -> 26.9 us
  starting transfers between devices: 34.1 us -> 30.1 us
    ppermute x29 -> x26, waiting for transfers between devices: 65.6 us -> 35.8 us  [moved(): return lax.ppermute(x, 'tm', pairs)]
    all_to_all x0 -> x2, blocking collectives: none -> 26.9 us  [on_device(): pieces = lax.all_to_all(pieces, 'tm', 0, 0, axis_index_groups=groups)]
    ppermute x29 -> x26, starting transfers between devices: 34.1 us -> 30.1 us  [moved(): return lax.ppermute(x, 'tm', pairs)]
    pallas_call x10 -> x11, Pallas kernels: 26.7 us -> 26.9 us  [kernel_call(): pl.pallas_call(body, out_shape=[jax.ShapeDtypeStruct(shape, jnp.float32)...]
  transfers between devices with their start and end apart: 29 -> 26, of which waited for: 20 -> 10; matrix products, arithmetic and copies ran while one was open for 0% -> 0% of each run, Pallas kernels for 5% -> 13%
where the time goes in v2:
time: 122 us
  waiting for transfers between devices  35.8 us (29%)
  starting transfers between devices  30.1 us (25%)
  Pallas kernels  26.9 us (22%)
  blocking collectives  26.9 us (22%)
  local copies, waits for them, and re-layouts  1.3 us (1%)
    ppermute x26, waiting for transfers between devices, moved(): return lax.ppermute(x, 'tm', pairs)  35.8 us
    ppermute x26, starting transfers between devices, moved(): return lax.ppermute(x, 'tm', pairs)  30.1 us
    all_to_all x2, blocking collectives, on_device(): pieces = lax.all_to_all(pieces, 'tm', 0, 0, axis_index_groups=groups)  26.9 us
    pallas_call x11, Pallas kernels, kernel_call(): pl.pallas_call(body, out_shape=[jax.ShapeDtypeStruct(shape, jnp.float32)...  26.9 us
  transfers between devices with their start and end apart: 26, of which 10 were waited for; matrix products, arithmetic and copies ran while one was open for 0% of the time, Pallas kernels for 13%

profile of v2, /device:TPU:1, one launch (start us, length us, event | category | flops | bytes accessed | tf_op | source)
XLA Modules:
  0.0 122.0 jit_solution(13906733037242015019)
XLA Ops:
  0.6 1.5 %collective-permute-start = (f32[512,512]{1,0:T(8,128)}, f32[512,512]{1,0:T(8,128)S(1)}, u32[]{:S(2)}, u32[]{:S(2)}) collective-permute-start(f32[512,512]{1,0:T(8,128)} %bitcast.6), channel_id=1, source_target_pairs={{4,0},{0,4},{12,8},{8,12},{20,16},{16,20},{28,24},{24,28},{36,32},... | collective-permute-start | bytes 3145736 | tf_op jit(solution)/shard_map/T_chip/ppermute | solution.py:27
  2.1 0.1 collective-permute-start.5
  2.2 2.4 %collective-permute-done.gain_other = f32[512,512]{1,0:T(8,128)S(1)} collective-permute-done((f32[512,512]{1,0:T(8,128)}, f32[512,512]{1,0:T(8,128)S(1)}, u32[]{:S(2)}, u32[]{:S(2)}) %collective-permute-start) | collective-permute-done | bytes 1048608 | tf_op jit(solution)/shard_map/T_chip/ppermute | solution.py:27
  4.6 1.2 %copy-done = f32[1,512,512]{2,1,0:T(8,128)S(1)} copy-done((f32[1,512,512]{2,1,0:T(8,128)S(1)}, f32[1,512,512]{2,1,0:T(8,128)}, u32[]{:S(2)}) %copy-start) | copy-done | bytes 1048600
  5.9 1.2 T_chip.2
  7.1 2.9 %collective-permute-start.1 = (f32[256,512]{1,0:T(8,128)S(1)}, f32[256,512]{1,0:T(8,128)S(1)}, u32[]{:S(2)}, u32[]{:S(2)}) collective-permute-start(f32[256,512]{1,0:T(8,128)S(1)} %get-tuple-element.29), channel_id=1, source_target_pairs={{8,0},{12,4},{16,8},{20,12},{24,16},{28,20},{0,24},{4,28},{40,32},... | collective-permute-start | bytes 1572872 | tf_op jit(solution)/shard_map/T_row/ppermute | solution.py:27
  10.0 0.0 collective-permute-start.3
  10.0 0.0 collective-permute-done.5.noise_other
  10.0 2.1 %T_chip.3 = (f32[512,512]{1,0:T(8,128)S(1)}, f32[136,512]{1,0:T(8,128)S(1)}) custom-call(f32[512,512]{1,0:T(8,128)S(1)} %bitcast.8, f32[512,512]{1,0:T(8,128)S(1)} %bitcast.11, f32[512,512]{1,0:T(8,128)S(1)} %collective-permute-done.gain_other, f32[512,512]{1,0:T(8,128)S(1)} %collective-permute-done.5.noise_other), custom_call_target="tpu_custom_call" | custom-call | flops 1610612736 | bytes 6291456 | tf_op jit(solution)/shard_map/T_chip/pallas_call | solution.py:69
  12.1 2.7 %collective-permute-start.6 = (f32[136,512]{1,0:T(8,128)S(1)}, f32[136,512]{1,0:T(8,128)S(1)}, u32[]{:S(2)}, u32[]{:S(2)}) collective-permute-start(f32[136,512]{1,0:T(8,128)S(1)} %get-tuple-element.30), channel_id=1, source_target_pairs={{8,0},{12,4},{16,8},{20,12},{24,16},{28,20},{0,24},{4,28},{40,32},... | collective-permute-start | bytes 835592 | tf_op jit(solution)/shard_map/T_row/ppermute | solution.py:27
  14.9 0.0 collective-permute-start.9
  14.9 12.0 %collective-permute-done.6.refs_0_ = f32[136,512]{1,0:T(8,128)S(1)} collective-permute-done((f32[136,512]{1,0:T(8,128)S(1)}, f32[136,512]{1,0:T(8,128)S(1)}, u32[]{:S(2)}, u32[]{:S(2)}) %collective-permute-start.6) | collective-permute-done | bytes 278560 | tf_op jit(solution)/shard_map/T_row/ppermute | solution.py:27
  26.9 3.1 %collective-permute-done.9.refs_2_ = f32[136,512]{1,0:T(8,128)S(1)} collective-permute-done((f32[136,512]{1,0:T(8,128)S(1)}, f32[136,512]{1,0:T(8,128)S(1)}, u32[]{:S(2)}, u32[]{:S(2)}) %collective-permute-start.9) | collective-permute-done | bytes 278560 | tf_op jit(solution)/shard_map/T_row/ppermute | solution.py:27
  30.0 0.0 collective-permute-done.1.refs_0_
  30.1 0.4 collective-permute-start.7
  30.5 0.0 collective-permute-done.3.refs_2_
  30.6 1.2 collective-permute-start.10
  31.7 2.1 %collective-permute-start.2 = (f32[256,512]{1,0:T(8,128)S(1)}, f32[256,512]{1,0:T(8,128)S(1)}, u32[]{:S(2)}, u32[]{:S(2)}) collective-permute-start(f32[256,512]{1,0:T(8,128)S(1)} %collective-permute-done.1.refs_0_), channel_id=1, source_target_pairs={{4,0},{0,4},{12,8},{8,12},{20,16},{16,20},{28,24},{24,28},{36,32},... | collective-permute-start | bytes 1572872 | tf_op jit(solution)/shard_map/T_row/ppermute | solution.py:27
  33.8 0.0 collective-permute-start.4
  33.8 5.8 %collective-permute-done.7.refs_4_ = f32[200,512]{1,0:T(8,128)S(1)} collective-permute-done((f32[200,512]{1,0:T(8,128)S(1)}, f32[200,512]{1,0:T(8,128)S(1)}, u32[]{:S(2)}, u32[]{:S(2)}) %collective-permute-start.7) | collective-permute-done | bytes 409632 | tf_op jit(solution)/shard_map/T_row/ppermute | solution.py:27
  39.6 2.4 %collective-permute-start.8 = (f32[200,512]{1,0:T(8,128)S(1)}, f32[200,512]{1,0:T(8,128)S(1)}, u32[]{:S(2)}, u32[]{:S(2)}) collective-permute-start(f32[200,512]{1,0:T(8,128)S(1)} %collective-permute-done.7.refs_4_), channel_id=1, source_target_pairs={{4,0},{0,4},{12,8},{8,12},{20,16},{16,20},{28,24},{24,28},{36,32},... | collective-permute-start | bytes 1228808 | tf_op jit(solution)/shard_map/T_row/ppermute | solution.py:27
  42.0 0.0 collective-permute-done.10.refs_6_
  42.0 1.3 %collective-permute-start.11 = (f32[192,512]{1,0:T(8,128)S(1)}, f32[192,512]{1,0:T(8,128)S(1)}, u32[]{:S(2)}, u32[]{:S(2)}) collective-permute-start(f32[192,512]{1,0:T(8,128)S(1)} %collective-permute-done.10.refs_6_), channel_id=1, source_target_pairs={{4,0},{0,4},{12,8},{8,12},{20,16},{16,20},{28,24},{24,28},{36,32},... | collective-permute-start | bytes 1179656 | tf_op jit(solution)/shard_map/T_row/ppermute | solution.py:27
  43.4 0.0 collective-permute-start.12
  43.4 0.0 collective-permute-done.2.refs_1_
  43.4 0.5 collective-permute-start.13
  43.9 0.0 collective-permute-done.4.refs_3_
  43.9 0.8 collective-permute-done.11.refs_7_
  44.7 0.0 collective-permute-done.8.refs_5_
  44.7 3.5 %T_row.2 = (bf16[3,512,512]{2,1,0:T(8,128)(2,1)S(1)}, bf16[3,512,512]{2,1,0:T(8,128)(2,1)S(1)}, f32[512,512]{1,0:T(8,128)S(1)}, f32[512,512]{1,0:T(8,128)S(1)}, f32[256,512]{1,0:T(8,128)S(1)}) custom-call(f32[512,512]{1,0:T(8,128)S(1)} %get-tuple-element.28.own, f32[256,512]{1,0:T(8,128)S(1)} %collective-permute-done.1.refs_0_, ...), custom_call_target="tpu_custom_call" | custom-call | flops 2415919104 | bytes 10485760 | tf_op jit(solution)/shard_map/T_row/pallas_call | solution.py:69
  48.2 0.0 collective-permute-done.12.refs_1_
  48.2 0.0 collective-permute-done.13.refs_3_
  48.2 0.0 copy-start.1
  48.2 0.0 copy-start.3
  48.2 6.4 %T_row.3 = (f32[512,512]{1,0:T(8,128)S(1)}, f32[512,512]{1,0:T(8,128)S(1)}, f32[136,512]{1,0:T(8,128)S(1)}) custom-call(bf16[3,512,512]{2,1,0:T(8,128)(2,1)S(1)} %get-tuple-element.31.high_ref, bf16[3,512,512]{2,1,0:T(8,128)(2,1)S(1)} %get-tuple-element.32.low_ref, f32[512,512]{1,0:T(8,128)S(1)} %get-tuple-element.33.own, ...), custom_call_target="tpu_custom_call" | custom-call | flops 4831838208 | bytes 8388608 | tf_op jit(solution)/shard_map/T_row/pallas_call | solution.py:69
  54.7 0.7 collective-permute-start.14
  55.3 1.3 %collective-permute-start.20 = (f32[256,512]{1,0:T(8,128)S(1)}, f32[256,512]{1,0:T(8,128)S(1)}, u32[]{:S(2)}, u32[]{:S(2)}) collective-permute-start(f32[256,512]{1,0:T(8,128)S(1)} %get-tuple-element.47), channel_id=1, source_target_pairs={{32,0},{36,4},{40,8},{44,12},{48,16},{52,20},{56,24},{60,28},{33,1... | collective-permute-start | bytes 1572872 | tf_op jit(solution)/shard_map/T_z/ppermute | solution.py:27
  56.7 4.6 %T_z.4 = (f32[512,512]{1,0:T(8,128)S(1)}, f32[512,512]{1,0:T(8,128)S(1)}, f32[512,512]{1,0:T(8,128)S(1)}, f32[512,512]{1,0:T(8,128)S(1)}) custom-call(f32[512,512]{1,0:T(8,128)S(1)} %get-tuple-element.35.after_gain, f32[512,512]{1,0:T(8,128)S(1)} %get-tuple-element.36.after_noise, f32[512,512]{1,0:T(8,128)S(1)} %bitcast.9, ...), custom_call_target="tpu_custom_call" | custom-call | flops 6442450944 | bytes 11534336 | tf_op jit(solution)/shard_map/T_z/pallas_call | solution.py:69
  61.3 2.9 %collective-permute-start.15 = (f32[136,512]{1,0:T(8,128)S(1)}, f32[136,512]{1,0:T(8,128)S(1)}, u32[]{:S(2)}, u32[]{:S(2)}) collective-permute-start(f32[136,512]{1,0:T(8,128)S(1)} %collective-permute-done.14.mine), channel_id=1, source_target_pairs={{4,0},{0,4},{12,8},{8,12},{20,16},{16,20},{28,24},{24,28},{36,32},... | collective-permute-start | bytes 835592 | tf_op jit(solution)/shard_map/T_z/ppermute | solution.py:27
  64.2 1.3 %collective-permute-start.22 = (f32[136,512]{1,0:T(8,128)S(1)}, f32[136,512]{1,0:T(8,128)S(1)}, u32[]{:S(2)}, u32[]{:S(2)}) collective-permute-start(f32[136,512]{1,0:T(8,128)S(1)} %get-tuple-element.34), channel_id=1, source_target_pairs={{32,0},{36,4},{40,8},{44,12},{48,16},{52,20},{56,24},{60,28},{33,1... | collective-permute-start | bytes 835592 | tf_op jit(solution)/shard_map/T_z/ppermute | solution.py:27
  65.5 0.0 collective-permute-done.15.other
  65.5 1.9 %T_z.5 = (f32[512,512]{1,0:T(8,128)S(1)}, f32[136,512]{1,0:T(8,128)S(1)}) custom-call(f32[136,512]{1,0:T(8,128)S(1)} %collective-permute-done.14.mine, f32[136,512]{1,0:T(8,128)S(1)} %collective-permute-done.15.other, f32[512,512]{1,0:T(8,128)S(1)} %get-tuple-element.44.gain, f32[512,512]{1,0:T(8,128)S(1)} %get-tuple-element.45.noise), custom_call_target="tpu_custom_call" | custom-call | flops 1610612736 | bytes 4194304 | tf_op jit(solution)/shard_map/T_z/pallas_call | solution.py:69
  67.5 0.7 collective-permute-start.16
  68.2 1.3 %collective-permute-start.18 = (f32[136,512]{1,0:T(8,128)S(1)}, f32[136,512]{1,0:T(8,128)S(1)}, u32[]{:S(2)}, u32[]{:S(2)}) collective-permute-start(f32[136,512]{1,0:T(8,128)S(1)} %get-tuple-element.46), channel_id=1, source_target_pairs={{64,0},{68,4},{72,8},{76,12},{80,16},{84,20},{88,24},{92,28},{65,1... | collective-permute-start | bytes 835592 | tf_op jit(solution)/shard_map/T_z/ppermute | solution.py:27
  69.5 0.9 collective-permute-done.20.lead
  70.4 2.0 %collective-permute-start.21 = (f32[256,512]{1,0:T(8,128)S(1)}, f32[256,512]{1,0:T(8,128)S(1)}, u32[]{:S(2)}, u32[]{:S(2)}) collective-permute-start(f32[256,512]{1,0:T(8,128)S(1)} %collective-permute-done.20.lead), channel_id=1, source_target_pairs={{4,0},{0,4},{12,8},{8,12},{20,16},{16,20},{28,24},{24,28},{36,32},... | collective-permute-start | bytes 1572872 | tf_op jit(solution)/shard_map/T_z/ppermute | solution.py:27
  72.4 4.0 %collective-permute-done.22.first = f32[136,512]{1,0:T(8,128)S(1)} collective-permute-done((f32[136,512]{1,0:T(8,128)S(1)}, f32[136,512]{1,0:T(8,128)S(1)}, u32[]{:S(2)}, u32[]{:S(2)}) %collective-permute-start.22) | collective-permute-done | bytes 278560 | tf_op jit(solution)/shard_map/T_z/ppermute | solution.py:27
  76.3 1.2 collective-permute-start.23
  77.5 0.0 collective-permute-start.17
  77.5 4.0 %collective-permute-done.18.far = f32[136,512]{1,0:T(8,128)S(1)} collective-permute-done((f32[136,512]{1,0:T(8,128)S(1)}, f32[136,512]{1,0:T(8,128)S(1)}, u32[]{:S(2)}, u32[]{:S(2)}) %collective-permute-start.18) | collective-permute-done | bytes 278560 | tf_op jit(solution)/shard_map/T_z/ppermute | solution.py:27
  81.6 1.0 collective-permute-start.19
  82.5 0.0 collective-permute-done.23.first_other
  82.6 0.0 collective-permute-done.21.lead_other
  82.6 1.2 collective-permute-done.19.far_other
  83.7 3.9 %T_z.6 = (f32[512,512]{1,0:T(8,128)S(1)}, f32[256,512]{1,0:T(8,128)S(1)}, f32[256,512]{1,0:T(8,128)S(1)}) custom-call(f32[136,512]{1,0:T(8,128)S(1)} %collective-permute-done.16.near, f32[136,512]{1,0:T(8,128)S(1)} %collective-permute-done.17.near_other, f32[136,512]{1,0:T(8,128)S(1)} %collective-permute-done.18.far, ...), custom_call_target="tpu_custom_call" | custom-call | flops 3221225472 | bytes 10485760 | tf_op jit(solution)/shard_map/T_z/pallas_call | solution.py:69
  87.7 0.5 collective-permute-start.24
  88.2 1.5 %collective-permute-done.24.given = f32[256,512]{1,0:T(8,128)S(1)} collective-permute-done((f32[256,512]{1,0:T(8,128)S(1)}, f32[256,512]{1,0:T(8,128)S(1)}, u32[]{:S(2)}, u32[]{:S(2)}) %collective-permute-start.24) | collective-permute-done | bytes 524320 | tf_op jit(solution)/shard_map/T_reduce/ppermute | solution.py:27
  89.7 0.1 T_reduce.3
  89.7 13.6 %all_to_all.10.refs_0_ = f32[16,16,512]{2,1,0:T(8,128)S(1)} all-to-all(f32[16,16,512]{2,1,0:T(8,128)S(1)} %T_reduce.3), channel_id=1, replica_groups={{0,8,16,24,32,40,48,56,64,72,80,88,96,104,112,120},{4,12,20,28,36,44,52..., dimensions={0} | all-to-all | bytes 1048576 | tf_op jit(solution)/shard_map/T_reduce/all_to_all | solution.py:412
  103.4 0.1 T_reduce.4
  103.4 13.3 %all_to_all.11 = f32[16,16,512]{2,1,0:T(8,128)S(1)} all-to-all(f32[16,16,512]{2,1,0:T(8,128)S(1)} %T_reduce.4), channel_id=1, replica_groups={{0,8,16,24,32,40,48,56,64,72,80,88,96,104,112,120},{4,12,20,28,36,44,52..., dimensions={0} | all-to-all | bytes 1048576 | tf_op jit(solution)/shard_map/T_reduce/all_to_all | solution.py:417
  116.8 2.2 %collective-permute-start.25 = (f32[256,512]{1,0:T(8,128)S(1)}, f32[256,512]{1,0:T(8,128)S(1)}, u32[]{:S(2)}, u32[]{:S(2)}) collective-permute-start(f32[256,512]{1,0:T(8,128)S(1)} %bitcast.4), channel_id=1, source_target_pairs={{4,0},{0,4},{12,8},{8,12},{20,16},{16,20},{28,24},{24,28},{36,32},... | collective-permute-start | bytes 1572872 | tf_op jit(solution)/shard_map/T_reduce/ppermute | solution.py:27
  118.9 2.0 %T_z.7 = f32[512,512]{1,0:T(8,128)} custom-call(f32[512,512]{1,0:T(8,128)S(1)} %get-tuple-element.41.from_gain, f32[512,512]{1,0:T(8,128)S(1)} %get-tuple-element.42.from_noise, f32[512,512]{1,0:T(8,128)S(1)} %get-tuple-element.51.carried), custom_call_target="tpu_custom_call" | custom-call | flops 805306368 | bytes 4194304 | tf_op jit(solution)/shard_map/T_z/pallas_call | solution.py:69
  120.9 1.1 T_reduce.5
  (15 shorter events, 0.1 us)
Async XLA Ops:
  0.6 4.0 %collective-permute-start = (f32[512,512]{1,0:T(8,128)}, f32[512,512]{1,0:T(8,128)S(1)}, u32[]{:S(2)}, u32[]{:S(2)}) collective-permute-start(f32[512,512]{1,0:T(8,128)} %bitcast.6), channel_id=1, source_target_pairs={{4,0},{0,4},{12,8},{8,12},{20,16},{16,20},{28,24},{24,28},{36,32},... | collective-permute-start | bytes 3145736 | tf_op jit(solution)/shard_map/T_chip/ppermute | solution.py:27
  2.1 7.8 %collective-permute-start.5 = (f32[512,512]{1,0:T(8,128)}, f32[512,512]{1,0:T(8,128)S(1)}, u32[]{:S(2)}, u32[]{:S(2)}) collective-permute-start(f32[512,512]{1,0:T(8,128)} %bitcast.10), channel_id=1, source_target_pairs={{4,0},{0,4},{12,8},{8,12},{20,16},{16,20},{28,24},{24,28},{36,32},... | collective-permute-start | bytes 3145736 | tf_op jit(solution)/shard_map/T_chip/ppermute | solution.py:27
  4.6 1.2 %copy-start = (f32[1,512,512]{2,1,0:T(8,128)S(1)}, f32[1,512,512]{2,1,0:T(8,128)}, u32[]{:S(2)}) copy-start(f32[1,512,512]{2,1,0:T(8,128)} %param.3) | copy-start | bytes 3145732
  5.9 4.1 %copy-start.2 = (f32[1,512,512]{2,1,0:T(8,128)S(1)}, f32[1,512,512]{2,1,0:T(8,128)}, u32[]{:S(2)}) copy-start(f32[1,512,512]{2,1,0:T(8,128)} %param.4) | copy-start | bytes 3145732
  7.1 22.9 %collective-permute-start.1 = (f32[256,512]{1,0:T(8,128)S(1)}, f32[256,512]{1,0:T(8,128)S(1)}, u32[]{:S(2)}, u32[]{:S(2)}) collective-permute-start(f32[256,512]{1,0:T(8,128)S(1)} %get-tuple-element.29), channel_id=1, source_target_pairs={{8,0},{12,4},{16,8},{20,12},{24,16},{28,20},{0,24},{4,28},{40,32},... | collective-permute-start | bytes 1572872 | tf_op jit(solution)/shard_map/T_row/ppermute | solution.py:27
  10.0 20.5 %collective-permute-start.3 = (f32[256,512]{1,0:T(8,128)S(1)}, f32[256,512]{1,0:T(8,128)S(1)}, u32[]{:S(2)}, u32[]{:S(2)}) collective-permute-start(f32[256,512]{1,0:T(8,128)S(1)} %get-tuple-element.29), channel_id=1, source_target_pairs={{24,0},{28,4},{0,8},{4,12},{8,16},{12,20},{16,24},{20,28},{56,32},... | collective-permute-start | bytes 1572872 | tf_op jit(solution)/shard_map/T_row/ppermute | solution.py:27
  12.1 14.8 %collective-permute-start.6 = (f32[136,512]{1,0:T(8,128)S(1)}, f32[136,512]{1,0:T(8,128)S(1)}, u32[]{:S(2)}, u32[]{:S(2)}) collective-permute-start(f32[136,512]{1,0:T(8,128)S(1)} %get-tuple-element.30), channel_id=1, source_target_pairs={{8,0},{12,4},{16,8},{20,12},{24,16},{28,20},{0,24},{4,28},{40,32},... | collective-permute-start | bytes 835592 | tf_op jit(solution)/shard_map/T_row/ppermute | solution.py:27
  14.9 15.1 %collective-permute-start.9 = (f32[136,512]{1,0:T(8,128)S(1)}, f32[136,512]{1,0:T(8,128)S(1)}, u32[]{:S(2)}, u32[]{:S(2)}) collective-permute-start(f32[136,512]{1,0:T(8,128)S(1)} %get-tuple-element.30), channel_id=1, source_target_pairs={{24,0},{28,4},{0,8},{4,12},{8,16},{12,20},{16,24},{20,28},{56,32},... | collective-permute-start | bytes 835592 | tf_op jit(solution)/shard_map/T_row/ppermute | solution.py:27
  30.1 9.5 %collective-permute-start.7 = (f32[200,512]{1,0:T(8,128)S(1)}, f32[200,512]{1,0:T(8,128)S(1)}, u32[]{:S(2)}, u32[]{:S(2)}) collective-permute-start(f32[200,512]{1,0:T(8,128)S(1)} %pad_maximum_fusion), channel_id=1, source_target_pairs={{8,0},{12,4},{16,8},{20,12},{24,16},{28,20},{0,24},{4,28},{40,32},... | collective-permute-start | bytes 1228808 | tf_op jit(solution)/shard_map/T_row/ppermute | solution.py:27
  30.6 11.5 %collective-permute-start.10 = (f32[192,512]{1,0:T(8,128)S(1)}, f32[192,512]{1,0:T(8,128)S(1)}, u32[]{:S(2)}, u32[]{:S(2)}) collective-permute-start(f32[192,512]{1,0:T(8,128)S(1)} %pad_maximum_fusion.1), channel_id=1, source_target_pairs={{24,0},{28,4},{0,8},{4,12},{8,16},{12,20},{16,24},{20,28},{56,32},... | collective-permute-start | bytes 1179656 | tf_op jit(solution)/shard_map/T_row/ppermute | solution.py:27
  31.7 11.6 %collective-permute-start.2 = (f32[256,512]{1,0:T(8,128)S(1)}, f32[256,512]{1,0:T(8,128)S(1)}, u32[]{:S(2)}, u32[]{:S(2)}) collective-permute-start(f32[256,512]{1,0:T(8,128)S(1)} %collective-permute-done.1.refs_0_), channel_id=1, source_target_pairs={{4,0},{0,4},{12,8},{8,12},{20,16},{16,20},{28,24},{24,28},{36,32},... | collective-permute-start | bytes 1572872 | tf_op jit(solution)/shard_map/T_row/ppermute | solution.py:27
  33.8 10.1 %collective-permute-start.4 = (f32[256,512]{1,0:T(8,128)S(1)}, f32[256,512]{1,0:T(8,128)S(1)}, u32[]{:S(2)}, u32[]{:S(2)}) collective-permute-start(f32[256,512]{1,0:T(8,128)S(1)} %collective-permute-done.3.refs_2_), channel_id=1, source_target_pairs={{4,0},{0,4},{12,8},{8,12},{20,16},{16,20},{28,24},{24,28},{36,32},... | collective-permute-start | bytes 1572872 | tf_op jit(solution)/shard_map/T_row/ppermute | solution.py:27
  39.6 5.1 %collective-permute-start.8 = (f32[200,512]{1,0:T(8,128)S(1)}, f32[200,512]{1,0:T(8,128)S(1)}, u32[]{:S(2)}, u32[]{:S(2)}) collective-permute-start(f32[200,512]{1,0:T(8,128)S(1)} %collective-permute-done.7.refs_4_), channel_id=1, source_target_pairs={{4,0},{0,4},{12,8},{8,12},{20,16},{16,20},{28,24},{24,28},{36,32},... | collective-permute-start | bytes 1228808 | tf_op jit(solution)/shard_map/T_row/ppermute | solution.py:27
  42.0 2.7 %collective-permute-start.11 = (f32[192,512]{1,0:T(8,128)S(1)}, f32[192,512]{1,0:T(8,128)S(1)}, u32[]{:S(2)}, u32[]{:S(2)}) collective-permute-start(f32[192,512]{1,0:T(8,128)S(1)} %collective-permute-done.10.refs_6_), channel_id=1, source_target_pairs={{4,0},{0,4},{12,8},{8,12},{20,16},{16,20},{28,24},{24,28},{36,32},... | collective-permute-start | bytes 1179656 | tf_op jit(solution)/shard_map/T_row/ppermute | solution.py:27
  43.4 4.8 %collective-permute-start.12 = (f32[136,512]{1,0:T(8,128)S(1)}, f32[136,512]{1,0:T(8,128)S(1)}, u32[]{:S(2)}, u32[]{:S(2)}) collective-permute-start(f32[136,512]{1,0:T(8,128)S(1)} %collective-permute-done.6.refs_0_), channel_id=1, source_target_pairs={{4,0},{0,4},{12,8},{8,12},{20,16},{16,20},{28,24},{24,28},{36,32},... | collective-permute-start | bytes 835592 | tf_op jit(solution)/shard_map/T_row/ppermute | solution.py:27
  43.4 4.8 %collective-permute-start.13 = (f32[136,512]{1,0:T(8,128)S(1)}, f32[136,512]{1,0:T(8,128)S(1)}, u32[]{:S(2)}, u32[]{:S(2)}) collective-permute-start(f32[136,512]{1,0:T(8,128)S(1)} %collective-permute-done.9.refs_2_), channel_id=1, source_target_pairs={{4,0},{0,4},{12,8},{8,12},{20,16},{16,20},{28,24},{24,28},{36,32},... | collective-permute-start | bytes 835592 | tf_op jit(solution)/shard_map/T_row/ppermute | solution.py:27
  48.2 8.4 %copy-start.1 = (f32[1,512,512]{2,1,0:T(8,128)S(1)}, f32[1,512,512]{2,1,0:T(8,128)}, u32[]{:S(2)}) copy-start(f32[1,512,512]{2,1,0:T(8,128)} %param.3) | copy-start | bytes 3145732
  48.2 8.4 %copy-start.3 = (f32[512,512]{1,0:T(8,128)S(1)}, f32[512,512]{1,0:T(8,128)}, u32[]{:S(2)}) copy-start(f32[512,512]{1,0:T(8,128)} %estimate.1) | copy-start | bytes 3145732
  54.7 6.7 %collective-permute-start.14 = (f32[136,512]{1,0:T(8,128)S(1)}, f32[136,512]{1,0:T(8,128)S(1)}, u32[]{:S(2)}, u32[]{:S(2)}) collective-permute-start(f32[136,512]{1,0:T(8,128)S(1)} %get-tuple-element.34), channel_id=1, source_target_pairs={{96,64},{100,68},{104,72},{108,76},{112,80},{116,84},{120,88},{124... | collective-permute-start | bytes 835592 | tf_op jit(solution)/shard_map/T_z/ppermute | solution.py:27
  55.3 15.0 %collective-permute-start.20 = (f32[256,512]{1,0:T(8,128)S(1)}, f32[256,512]{1,0:T(8,128)S(1)}, u32[]{:S(2)}, u32[]{:S(2)}) collective-permute-start(f32[256,512]{1,0:T(8,128)S(1)} %get-tuple-element.47), channel_id=1, source_target_pairs={{32,0},{36,4},{40,8},{44,12},{48,16},{52,20},{56,24},{60,28},{33,1... | collective-permute-start | bytes 1572872 | tf_op jit(solution)/shard_map/T_z/ppermute | solution.py:27
  61.3 4.2 %collective-permute-start.15 = (f32[136,512]{1,0:T(8,128)S(1)}, f32[136,512]{1,0:T(8,128)S(1)}, u32[]{:S(2)}, u32[]{:S(2)}) collective-permute-start(f32[136,512]{1,0:T(8,128)S(1)} %collective-permute-done.14.mine), channel_id=1, source_target_pairs={{4,0},{0,4},{12,8},{8,12},{20,16},{16,20},{28,24},{24,28},{36,32},... | collective-permute-start | bytes 835592 | tf_op jit(solution)/shard_map/T_z/ppermute | solution.py:27
  64.2 12.1 %collective-permute-start.22 = (f32[136,512]{1,0:T(8,128)S(1)}, f32[136,512]{1,0:T(8,128)S(1)}, u32[]{:S(2)}, u32[]{:S(2)}) collective-permute-start(f32[136,512]{1,0:T(8,128)S(1)} %get-tuple-element.34), channel_id=1, source_target_pairs={{32,0},{36,4},{40,8},{44,12},{48,16},{52,20},{56,24},{60,28},{33,1... | collective-permute-start | bytes 835592 | tf_op jit(solution)/shard_map/T_z/ppermute | solution.py:27
  67.5 10.1 %collective-permute-start.16 = (f32[136,512]{1,0:T(8,128)S(1)}, f32[136,512]{1,0:T(8,128)S(1)}, u32[]{:S(2)}, u32[]{:S(2)}) collective-permute-start(f32[136,512]{1,0:T(8,128)S(1)} %get-tuple-element.46), channel_id=1, source_target_pairs={{64,32},{68,36},{72,40},{76,44},{80,48},{84,52},{88,56},{92,60},{6... | collective-permute-start | bytes 835592 | tf_op jit(solution)/shard_map/T_z/ppermute | solution.py:27
  68.2 13.4 %collective-permute-start.18 = (f32[136,512]{1,0:T(8,128)S(1)}, f32[136,512]{1,0:T(8,128)S(1)}, u32[]{:S(2)}, u32[]{:S(2)}) collective-permute-start(f32[136,512]{1,0:T(8,128)S(1)} %get-tuple-element.46), channel_id=1, source_target_pairs={{64,0},{68,4},{72,8},{76,12},{80,16},{84,20},{88,24},{92,28},{65,1... | collective-permute-start | bytes 835592 | tf_op jit(solution)/shard_map/T_z/ppermute | solution.py:27
  70.4 12.2 %collective-permute-start.21 = (f32[256,512]{1,0:T(8,128)S(1)}, f32[256,512]{1,0:T(8,128)S(1)}, u32[]{:S(2)}, u32[]{:S(2)}) collective-permute-start(f32[256,512]{1,0:T(8,128)S(1)} %collective-permute-done.20.lead), channel_id=1, source_target_pairs={{4,0},{0,4},{12,8},{8,12},{20,16},{16,20},{28,24},{24,28},{36,32},... | collective-permute-start | bytes 1572872 | tf_op jit(solution)/shard_map/T_z/ppermute | solution.py:27
  76.3 6.2 %collective-permute-start.23 = (f32[136,512]{1,0:T(8,128)S(1)}, f32[136,512]{1,0:T(8,128)S(1)}, u32[]{:S(2)}, u32[]{:S(2)}) collective-permute-start(f32[136,512]{1,0:T(8,128)S(1)} %collective-permute-done.22.first), channel_id=1, source_target_pairs={{4,0},{0,4},{12,8},{8,12},{20,16},{16,20},{28,24},{24,28},{36,32},... | collective-permute-start | bytes 835592 | tf_op jit(solution)/shard_map/T_z/ppermute | solution.py:27
  77.5 5.0 %collective-permute-start.17 = (f32[136,512]{1,0:T(8,128)S(1)}, f32[136,512]{1,0:T(8,128)S(1)}, u32[]{:S(2)}, u32[]{:S(2)}) collective-permute-start(f32[136,512]{1,0:T(8,128)S(1)} %collective-permute-done.16.near), channel_id=1, source_target_pairs={{4,0},{0,4},{12,8},{8,12},{20,16},{16,20},{28,24},{24,28},{36,32},... | collective-permute-start | bytes 835592 | tf_op jit(solution)/shard_map/T_z/ppermute | solution.py:27
  81.6 2.2 %collective-permute-start.19 = (f32[136,512]{1,0:T(8,128)S(1)}, f32[136,512]{1,0:T(8,128)S(1)}, u32[]{:S(2)}, u32[]{:S(2)}) collective-permute-start(f32[136,512]{1,0:T(8,128)S(1)} %collective-permute-done.18.far), channel_id=1, source_target_pairs={{4,0},{0,4},{12,8},{8,12},{20,16},{16,20},{28,24},{24,28},{36,32},... | collective-permute-start | bytes 835592 | tf_op jit(solution)/shard_map/T_z/ppermute | solution.py:27
  87.7 2.0 %collective-permute-start.24 = (f32[256,512]{1,0:T(8,128)S(1)}, f32[256,512]{1,0:T(8,128)S(1)}, u32[]{:S(2)}, u32[]{:S(2)}) collective-permute-start(f32[256,512]{1,0:T(8,128)S(1)} %get-tuple-element.53), channel_id=1, source_target_pairs={{4,0},{0,4},{12,8},{8,12},{20,16},{16,20},{28,24},{24,28},{36,32},... | collective-permute-start | bytes 1572872 | tf_op jit(solution)/shard_map/T_reduce/ppermute | solution.py:27
  116.8 4.2 %collective-permute-start.25 = (f32[256,512]{1,0:T(8,128)S(1)}, f32[256,512]{1,0:T(8,128)S(1)}, u32[]{:S(2)}, u32[]{:S(2)}) collective-permute-start(f32[256,512]{1,0:T(8,128)S(1)} %bitcast.4), channel_id=1, source_target_pairs={{4,0},{0,4},{12,8},{8,12},{20,16},{16,20},{28,24},{24,28},{36,32},... | collective-permute-start | bytes 1572872 | tf_op jit(solution)/shard_map/T_reduce/ppermute | solution.py:27

commit v3 on v2

--- a/solution.py
+++ b/solution.py
@@ -121,27 +121,21 @@
     return jnp.concatenate([top, jnp.concatenate([b.T, d], axis=1)], axis=0)
 
 
-def chip_gain_kernel(gain, gain_other, gain_ref, send_ref, g_ref, sems):
+def copy_kernel(gain, noise, gain_ref, noise_ref):
+    gain_ref[...], noise_ref[...] = gain[...], noise[...]
+
+
+def chip_gain_kernel(gain, gain_other, gain_ref, send_ref, g_ref):
     _, _, core = place()
-    copy = pltpu.make_async_copy(gain, g_ref.at[core], sems.at[0])
-    copy.start()
-    g_ref[1 - core] = gain_other[...]
-    copy.wait()
+    g_ref[core], g_ref[1 - core] = gain[...], gain_other[...]
     gain_ref[...] = dot3(split(g_ref[0]), split(g_ref[1]))
     send_ref[...] = gain_ref[rows_at(core, send_ref.shape[0]), :]
 
 
-def chip_noise_kernel(gain, noise, gain_other, noise_other, noise_ref, packed_ref, g_ref, n_ref, sems):
+def chip_noise_kernel(gain, noise, gain_other, noise_other, noise_ref, packed_ref, g_ref, n_ref):
     _, _, core = place()
-    copies = [
-        pltpu.make_async_copy(gain, g_ref.at[core], sems.at[0]),
-        pltpu.make_async_copy(noise, n_ref.at[core], sems.at[1]),
-    ]
-    for copy in copies:
-        copy.start()
-    g_ref[1 - core], n_ref[1 - core] = gain_other[...], noise_other[...]
-    for copy in copies:
-        copy.wait()
+    g_ref[core], g_ref[1 - core] = gain[...], gain_other[...]
+    n_ref[core], n_ref[1 - core] = noise[...], noise_other[...]
     result = carry(split(g_ref[0]), n_ref[1], n_ref[0])
     noise_ref[...] = result
     pack(result, packed_ref, 0, core)
@@ -328,8 +322,9 @@
 
     with jax.named_scope("T_chip"):
         gain_other, noise_other = swap_cores(gain), swap_cores(noise)
+        gain, noise = kernel_call(copy_kernel, [square] * 2, (gain, noise), (), 0, 4 * size)
         chip_gain, gain_mine = kernel_call(
-            chip_gain_kernel, [square, strip], (gain, gain_other), [(CORES, *square)], flops, 4 * size, 1
+            chip_gain_kernel, [square, strip], (gain, gain_other), [(CORES, *square)], flops, 4 * size
         )
         chip_noise, noise_mine = kernel_call(
             chip_noise_kernel,
@@ -338,7 +333,6 @@
             [(CORES, *square)] * 2,
             2 * flops,
             6 * size,
-            2,
         )
 
     with jax.named_scope("T_row"):

time: 122 us -> 121 us (level)
  waiting for transfers between devices: 35.8 us -> 33 us
    ppermute x26, waiting for transfers between devices: 35.8 us -> 33 us  [moved(): return lax.ppermute(x, 'tm', pairs)]
    unnamed x8 -> x6, local copies, waits for them, and re-layouts: 1.24 us -> 2.45 us
    pallas_call x11 -> x12, Pallas kernels: 26.9 us -> 27.4 us  [kernel_call(): pl.pallas_call(body, out_shape=[jax.ShapeDtypeStruct(shape, jnp.float32)...]
  transfers between devices with their start and end apart: 26 -> 26, of which waited for: 10 -> 8; matrix products, arithmetic and copies ran while one was open for 0% -> 0% of each run, Pallas kernels for 13% -> 13%
where the time goes in v3:
time: 121 us
  waiting for transfers between devices  33 us (27%)
  starting transfers between devices  30.3 us (25%)
  Pallas kernels  27.4 us (23%)
  blocking collectives  26.9 us (22%)
  local copies, waits for them, and re-layouts  2.51 us (2%)
    ppermute x26, waiting for transfers between devices, moved(): return lax.ppermute(x, 'tm', pairs)  33 us
    ppermute x26, starting transfers between devices, moved(): return lax.ppermute(x, 'tm', pairs)  30.3 us
    pallas_call x12, Pallas kernels, kernel_call(): pl.pallas_call(body, out_shape=[jax.ShapeDtypeStruct(shape, jnp.float32)...  27.4 us
    all_to_all x2, blocking collectives, on_device(): pieces = lax.all_to_all(pieces, 'tm', 0, 0, axis_index_groups=groups)  26.9 us
    unnamed x6, local copies, waits for them, and re-layouts  2.45 us
  transfers between devices with their start and end apart: 26, of which 8 were waited for; matrix products, arithmetic and copies ran while one was open for 0% of the time, Pallas kernels for 13%

profile of v3, /device:TPU:1, one launch (start us, length us, event | category | flops | bytes accessed | tf_op | source)
XLA Modules:
  0.0 121.1 jit_solution(4192946305914825985)
XLA Ops:
  0.6 1.5 %collective-permute-start = (f32[512,512]{1,0:T(8,128)}, f32[512,512]{1,0:T(8,128)S(1)}, u32[]{:S(2)}, u32[]{:S(2)}) collective-permute-start(f32[512,512]{1,0:T(8,128)} %bitcast.6), channel_id=1, source_target_pairs={{4,0},{0,4},{12,8},{8,12},{20,16},{16,20},{28,24},{24,28},{36,32},... | collective-permute-start | bytes 3145736 | tf_op jit(solution)/shard_map/T_chip/ppermute | solution.py:27
  2.1 0.1 collective-permute-start.5
  2.2 1.2 %copy-done = f32[1,512,512]{2,1,0:T(8,128)S(1)} copy-done((f32[1,512,512]{2,1,0:T(8,128)S(1)}, f32[1,512,512]{2,1,0:T(8,128)}, u32[]{:S(2)}) %copy-start) | copy-done | bytes 1048600
  3.5 1.2 %copy-done.1 = f32[1,512,512]{2,1,0:T(8,128)S(1)} copy-done((f32[1,512,512]{2,1,0:T(8,128)S(1)}, f32[1,512,512]{2,1,0:T(8,128)}, u32[]{:S(2)}) %copy-start.1) | copy-done | bytes 1048600
  4.7 0.1 T_chip.3
  4.8 0.0 collective-permute-done.gain_other
  4.8 1.5 %T_chip.4 = (f32[512,512]{1,0:T(8,128)S(1)}, f32[256,512]{1,0:T(8,128)S(1)}) custom-call(f32[512,512]{1,0:T(8,128)S(1)} %get-tuple-element.30.gain, f32[512,512]{1,0:T(8,128)S(1)} %collective-permute-done.gain_other), custom_call_target="tpu_custom_call" | custom-call | flops 805306368 | bytes 4194304 | tf_op jit(solution)/shard_map/T_chip/pallas_call | solution.py:69
  6.3 2.9 %collective-permute-start.1 = (f32[256,512]{1,0:T(8,128)S(1)}, f32[256,512]{1,0:T(8,128)S(1)}, u32[]{:S(2)}, u32[]{:S(2)}) collective-permute-start(f32[256,512]{1,0:T(8,128)S(1)} %get-tuple-element.32), channel_id=1, source_target_pairs={{8,0},{12,4},{16,8},{20,12},{24,16},{28,20},{0,24},{4,28},{40,32},... | collective-permute-start | bytes 1572872 | tf_op jit(solution)/shard_map/T_row/ppermute | solution.py:27
  9.2 0.0 collective-permute-start.3
  9.2 0.0 collective-permute-done.5.noise_other
  9.2 2.3 %T_chip.5 = (f32[512,512]{1,0:T(8,128)S(1)}, f32[136,512]{1,0:T(8,128)S(1)}) custom-call(f32[512,512]{1,0:T(8,128)S(1)} %get-tuple-element.30.gain, f32[512,512]{1,0:T(8,128)S(1)} %get-tuple-element.33.noise, f32[512,512]{1,0:T(8,128)S(1)} %collective-permute-done.gain_other, f32[512,512]{1,0:T(8,128)S(1)} %collective-permute-done.5.noise_other), custom_call_target="tpu_custom_call" | custom-call | flops 1610612736 | bytes 6291456 | tf_op jit(solution)/shard_map/T_chip/pallas_call | solution.py:69
  11.5 0.1 collective-permute-start.9
  11.6 2.7 %collective-permute-start.6 = (f32[136,512]{1,0:T(8,128)S(1)}, f32[136,512]{1,0:T(8,128)S(1)}, u32[]{:S(2)}, u32[]{:S(2)}) collective-permute-start(f32[136,512]{1,0:T(8,128)S(1)} %get-tuple-element.34), channel_id=1, source_target_pairs={{8,0},{12,4},{16,8},{20,12},{24,16},{28,20},{0,24},{4,28},{40,32},... | collective-permute-start | bytes 835592 | tf_op jit(solution)/shard_map/T_row/ppermute | solution.py:27
  14.3 14.8 %collective-permute-done.9.refs_2_ = f32[136,512]{1,0:T(8,128)S(1)} collective-permute-done((f32[136,512]{1,0:T(8,128)S(1)}, f32[136,512]{1,0:T(8,128)S(1)}, u32[]{:S(2)}, u32[]{:S(2)}) %collective-permute-start.9) | collective-permute-done | bytes 278560 | tf_op jit(solution)/shard_map/T_row/ppermute | solution.py:27
  29.1 0.0 collective-permute-done.6.refs_0_
  29.2 0.0 collective-permute-done.1.refs_0_
  29.2 0.4 collective-permute-start.7
  29.6 0.0 collective-permute-done.3.refs_2_
  29.7 1.2 %collective-permute-start.10 = (f32[192,512]{1,0:T(8,128)S(1)}, f32[192,512]{1,0:T(8,128)S(1)}, u32[]{:S(2)}, u32[]{:S(2)}) collective-permute-start(f32[192,512]{1,0:T(8,128)S(1)} %pad_maximum_fusion.1), channel_id=1, source_target_pairs={{24,0},{28,4},{0,8},{4,12},{8,16},{12,20},{16,24},{20,28},{56,32},... | collective-permute-start | bytes 1179656 | tf_op jit(solution)/shard_map/T_row/ppermute | solution.py:27
  30.9 2.1 %collective-permute-start.2 = (f32[256,512]{1,0:T(8,128)S(1)}, f32[256,512]{1,0:T(8,128)S(1)}, u32[]{:S(2)}, u32[]{:S(2)}) collective-permute-start(f32[256,512]{1,0:T(8,128)S(1)} %collective-permute-done.1.refs_0_), channel_id=1, source_target_pairs={{4,0},{0,4},{12,8},{8,12},{20,16},{16,20},{28,24},{24,28},{36,32},... | collective-permute-start | bytes 1572872 | tf_op jit(solution)/shard_map/T_row/ppermute | solution.py:27
  33.0 0.0 collective-permute-start.4
  33.0 5.7 %collective-permute-done.7.refs_4_ = f32[200,512]{1,0:T(8,128)S(1)} collective-permute-done((f32[200,512]{1,0:T(8,128)S(1)}, f32[200,512]{1,0:T(8,128)S(1)}, u32[]{:S(2)}, u32[]{:S(2)}) %collective-permute-start.7) | collective-permute-done | bytes 409632 | tf_op jit(solution)/shard_map/T_row/ppermute | solution.py:27
  38.7 2.5 %collective-permute-start.8 = (f32[200,512]{1,0:T(8,128)S(1)}, f32[200,512]{1,0:T(8,128)S(1)}, u32[]{:S(2)}, u32[]{:S(2)}) collective-permute-start(f32[200,512]{1,0:T(8,128)S(1)} %collective-permute-done.7.refs_4_), channel_id=1, source_target_pairs={{4,0},{0,4},{12,8},{8,12},{20,16},{16,20},{28,24},{24,28},{36,32},... | collective-permute-start | bytes 1228808 | tf_op jit(solution)/shard_map/T_row/ppermute | solution.py:27
  41.2 0.0 collective-permute-done.10.refs_6_
  41.2 1.3 %collective-permute-start.11 = (f32[192,512]{1,0:T(8,128)S(1)}, f32[192,512]{1,0:T(8,128)S(1)}, u32[]{:S(2)}, u32[]{:S(2)}) collective-permute-start(f32[192,512]{1,0:T(8,128)S(1)} %collective-permute-done.10.refs_6_), channel_id=1, source_target_pairs={{4,0},{0,4},{12,8},{8,12},{20,16},{16,20},{28,24},{24,28},{36,32},... | collective-permute-start | bytes 1179656 | tf_op jit(solution)/shard_map/T_row/ppermute | solution.py:27
  42.5 0.0 collective-permute-start.12
  42.5 0.0 collective-permute-done.2.refs_1_
  42.5 0.5 collective-permute-start.13
  43.0 0.0 collective-permute-done.4.refs_3_
  43.0 0.8 collective-permute-done.11.refs_7_
  43.8 0.0 collective-permute-done.8.refs_5_
  43.8 3.5 %T_row.2 = (bf16[3,512,512]{2,1,0:T(8,128)(2,1)S(1)}, bf16[3,512,512]{2,1,0:T(8,128)(2,1)S(1)}, f32[512,512]{1,0:T(8,128)S(1)}, f32[512,512]{1,0:T(8,128)S(1)}, f32[256,512]{1,0:T(8,128)S(1)}) custom-call(f32[512,512]{1,0:T(8,128)S(1)} %get-tuple-element.31.own, f32[256,512]{1,0:T(8,128)S(1)} %collective-permute-done.1.refs_0_, ...), custom_call_target="tpu_custom_call" | custom-call | flops 2415919104 | bytes 10485760 | tf_op jit(solution)/shard_map/T_row/pallas_call | solution.py:69
  47.3 0.0 collective-permute-done.12.refs_1_
  47.3 0.0 collective-permute-done.13.refs_3_
  47.3 0.0 copy-start.2
  47.4 6.4 %T_row.3 = (f32[512,512]{1,0:T(8,128)S(1)}, f32[512,512]{1,0:T(8,128)S(1)}, f32[136,512]{1,0:T(8,128)S(1)}) custom-call(bf16[3,512,512]{2,1,0:T(8,128)(2,1)S(1)} %get-tuple-element.35.high_ref, bf16[3,512,512]{2,1,0:T(8,128)(2,1)S(1)} %get-tuple-element.36.low_ref, f32[512,512]{1,0:T(8,128)S(1)} %get-tuple-element.37.own, ...), custom_call_target="tpu_custom_call" | custom-call | flops 4831838208 | bytes 8388608 | tf_op jit(solution)/shard_map/T_row/pallas_call | solution.py:69
  53.8 0.7 collective-permute-start.14
  54.4 1.3 %collective-permute-start.20 = (f32[256,512]{1,0:T(8,128)S(1)}, f32[256,512]{1,0:T(8,128)S(1)}, u32[]{:S(2)}, u32[]{:S(2)}) collective-permute-start(f32[256,512]{1,0:T(8,128)S(1)} %get-tuple-element.51), channel_id=1, source_target_pairs={{32,0},{36,4},{40,8},{44,12},{48,16},{52,20},{56,24},{60,28},{33,1... | collective-permute-start | bytes 1572872 | tf_op jit(solution)/shard_map/T_z/ppermute | solution.py:27
  55.8 4.6 %T_z.4 = (f32[512,512]{1,0:T(8,128)S(1)}, f32[512,512]{1,0:T(8,128)S(1)}, f32[512,512]{1,0:T(8,128)S(1)}, f32[512,512]{1,0:T(8,128)S(1)}) custom-call(f32[512,512]{1,0:T(8,128)S(1)} %get-tuple-element.39.after_gain, f32[512,512]{1,0:T(8,128)S(1)} %get-tuple-element.40.after_noise, f32[512,512]{1,0:T(8,128)S(1)} %get-tuple-element.30.gain, ...), custom_call_target="tpu_custom_call" | custom-call | flops 6442450944 | bytes 11534336 | tf_op jit(solution)/shard_map/T_z/pallas_call | solution.py:69
  60.4 0.0 collective-permute-done.14.mine
  60.4 2.9 %collective-permute-start.15 = (f32[136,512]{1,0:T(8,128)S(1)}, f32[136,512]{1,0:T(8,128)S(1)}, u32[]{:S(2)}, u32[]{:S(2)}) collective-permute-start(f32[136,512]{1,0:T(8,128)S(1)} %collective-permute-done.14.mine), channel_id=1, source_target_pairs={{4,0},{0,4},{12,8},{8,12},{20,16},{16,20},{28,24},{24,28},{36,32},... | collective-permute-start | bytes 835592 | tf_op jit(solution)/shard_map/T_z/ppermute | solution.py:27
  63.3 1.3 %collective-permute-start.22 = (f32[136,512]{1,0:T(8,128)S(1)}, f32[136,512]{1,0:T(8,128)S(1)}, u32[]{:S(2)}, u32[]{:S(2)}) collective-permute-start(f32[136,512]{1,0:T(8,128)S(1)} %get-tuple-element.38), channel_id=1, source_target_pairs={{32,0},{36,4},{40,8},{44,12},{48,16},{52,20},{56,24},{60,28},{33,1... | collective-permute-start | bytes 835592 | tf_op jit(solution)/shard_map/T_z/ppermute | solution.py:27
  64.6 1.9 %T_z.5 = (f32[512,512]{1,0:T(8,128)S(1)}, f32[136,512]{1,0:T(8,128)S(1)}) custom-call(f32[136,512]{1,0:T(8,128)S(1)} %collective-permute-done.14.mine, f32[136,512]{1,0:T(8,128)S(1)} %collective-permute-done.15.other, f32[512,512]{1,0:T(8,128)S(1)} %get-tuple-element.48.gain, f32[512,512]{1,0:T(8,128)S(1)} %get-tuple-element.49.noise), custom_call_target="tpu_custom_call" | custom-call | flops 1610612736 | bytes 4194304 | tf_op jit(solution)/shard_map/T_z/pallas_call | solution.py:69
  66.6 0.7 collective-permute-start.16
  67.3 1.3 %collective-permute-start.18 = (f32[136,512]{1,0:T(8,128)S(1)}, f32[136,512]{1,0:T(8,128)S(1)}, u32[]{:S(2)}, u32[]{:S(2)}) collective-permute-start(f32[136,512]{1,0:T(8,128)S(1)} %get-tuple-element.50), channel_id=1, source_target_pairs={{64,0},{68,4},{72,8},{76,12},{80,16},{84,20},{88,24},{92,28},{65,1... | collective-permute-start | bytes 835592 | tf_op jit(solution)/shard_map/T_z/ppermute | solution.py:27
  68.6 0.9 collective-permute-done.20.lead
  69.5 2.0 %collective-permute-start.21 = (f32[256,512]{1,0:T(8,128)S(1)}, f32[256,512]{1,0:T(8,128)S(1)}, u32[]{:S(2)}, u32[]{:S(2)}) collective-permute-start(f32[256,512]{1,0:T(8,128)S(1)} %collective-permute-done.20.lead), channel_id=1, source_target_pairs={{4,0},{0,4},{12,8},{8,12},{20,16},{16,20},{28,24},{24,28},{36,32},... | collective-permute-start | bytes 1572872 | tf_op jit(solution)/shard_map/T_z/ppermute | solution.py:27
  71.5 4.0 %collective-permute-done.22.first = f32[136,512]{1,0:T(8,128)S(1)} collective-permute-done((f32[136,512]{1,0:T(8,128)S(1)}, f32[136,512]{1,0:T(8,128)S(1)}, u32[]{:S(2)}, u32[]{:S(2)}) %collective-permute-start.22) | collective-permute-done | bytes 278560 | tf_op jit(solution)/shard_map/T_z/ppermute | solution.py:27
  75.5 1.2 collective-permute-start.23
  76.6 0.0 collective-permute-done.16.near
  76.7 0.0 collective-permute-start.17
  76.7 4.0 %collective-permute-done.18.far = f32[136,512]{1,0:T(8,128)S(1)} collective-permute-done((f32[136,512]{1,0:T(8,128)S(1)}, f32[136,512]{1,0:T(8,128)S(1)}, u32[]{:S(2)}, u32[]{:S(2)}) %collective-permute-start.18) | collective-permute-done | bytes 278560 | tf_op jit(solution)/shard_map/T_z/ppermute | solution.py:27
  80.7 1.0 collective-permute-start.19
  81.7 1.2 collective-permute-done.19.far_other
  82.8 3.9 %T_z.6 = (f32[512,512]{1,0:T(8,128)S(1)}, f32[256,512]{1,0:T(8,128)S(1)}, f32[256,512]{1,0:T(8,128)S(1)}) custom-call(f32[136,512]{1,0:T(8,128)S(1)} %collective-permute-done.16.near, f32[136,512]{1,0:T(8,128)S(1)} %collective-permute-done.17.near_other, f32[136,512]{1,0:T(8,128)S(1)} %collective-permute-done.18.far, ...), custom_call_target="tpu_custom_call" | custom-call | flops 3221225472 | bytes 10485760 | tf_op jit(solution)/shard_map/T_z/pallas_call | solution.py:69
  86.8 0.5 collective-permute-start.24
  87.3 1.5 %collective-permute-done.24.given = f32[256,512]{1,0:T(8,128)S(1)} collective-permute-done((f32[256,512]{1,0:T(8,128)S(1)}, f32[256,512]{1,0:T(8,128)S(1)}, u32[]{:S(2)}, u32[]{:S(2)}) %collective-permute-start.24) | collective-permute-done | bytes 524320 | tf_op jit(solution)/shard_map/T_reduce/ppermute | solution.py:27
  88.8 0.1 T_reduce.3
  88.9 13.6 %all_to_all.10.refs_0_ = f32[16,16,512]{2,1,0:T(8,128)S(1)} all-to-all(f32[16,16,512]{2,1,0:T(8,128)S(1)} %T_reduce.3), channel_id=1, replica_groups={{0,8,16,24,32,40,48,56,64,72,80,88,96,104,112,120},{4,12,20,28,36,44,52..., dimensions={0} | all-to-all | bytes 1048576 | tf_op jit(solution)/shard_map/T_reduce/all_to_all | solution.py:406
  102.5 0.1 T_reduce.4
  102.5 13.3 %all_to_all.11 = f32[16,16,512]{2,1,0:T(8,128)S(1)} all-to-all(f32[16,16,512]{2,1,0:T(8,128)S(1)} %T_reduce.4), channel_id=1, replica_groups={{0,8,16,24,32,40,48,56,64,72,80,88,96,104,112,120},{4,12,20,28,36,44,52..., dimensions={0} | all-to-all | bytes 1048576 | tf_op jit(solution)/shard_map/T_reduce/all_to_all | solution.py:411
  115.9 2.2 %collective-permute-start.25 = (f32[256,512]{1,0:T(8,128)S(1)}, f32[256,512]{1,0:T(8,128)S(1)}, u32[]{:S(2)}, u32[]{:S(2)}) collective-permute-start(f32[256,512]{1,0:T(8,128)S(1)} %bitcast.4), channel_id=1, source_target_pairs={{4,0},{0,4},{12,8},{8,12},{20,16},{16,20},{28,24},{24,28},{36,32},... | collective-permute-start | bytes 1572872 | tf_op jit(solution)/shard_map/T_reduce/ppermute | solution.py:27
  118.0 2.0 %T_z.7 = f32[512,512]{1,0:T(8,128)} custom-call(f32[512,512]{1,0:T(8,128)S(1)} %get-tuple-element.45.from_gain, f32[512,512]{1,0:T(8,128)S(1)} %get-tuple-element.46.from_noise, f32[512,512]{1,0:T(8,128)S(1)} %get-tuple-element.55.carried), custom_call_target="tpu_custom_call" | custom-call | flops 805306368 | bytes 4194304 | tf_op jit(solution)/shard_map/T_z/pallas_call | solution.py:69
  120.0 1.1 T_reduce.5
  (14 shorter events, 0.1 us)
Async XLA Ops:
  0.6 4.2 %collective-permute-start = (f32[512,512]{1,0:T(8,128)}, f32[512,512]{1,0:T(8,128)S(1)}, u32[]{:S(2)}, u32[]{:S(2)}) collective-permute-start(f32[512,512]{1,0:T(8,128)} %bitcast.6), channel_id=1, source_target_pairs={{4,0},{0,4},{12,8},{8,12},{20,16},{16,20},{28,24},{24,28},{36,32},... | collective-permute-start | bytes 3145736 | tf_op jit(solution)/shard_map/T_chip/ppermute | solution.py:27
  2.1 7.1 %collective-permute-start.5 = (f32[512,512]{1,0:T(8,128)}, f32[512,512]{1,0:T(8,128)S(1)}, u32[]{:S(2)}, u32[]{:S(2)}) collective-permute-start(f32[512,512]{1,0:T(8,128)} %bitcast.8), channel_id=1, source_target_pairs={{4,0},{0,4},{12,8},{8,12},{20,16},{16,20},{28,24},{24,28},{36,32},... | collective-permute-start | bytes 3145736 | tf_op jit(solution)/shard_map/T_chip/ppermute | solution.py:27
  2.2 1.2 %copy-start = (f32[1,512,512]{2,1,0:T(8,128)S(1)}, f32[1,512,512]{2,1,0:T(8,128)}, u32[]{:S(2)}) copy-start(f32[1,512,512]{2,1,0:T(8,128)} %param.3) | copy-start | bytes 3145732
  3.4 1.2 %copy-start.1 = (f32[1,512,512]{2,1,0:T(8,128)S(1)}, f32[1,512,512]{2,1,0:T(8,128)}, u32[]{:S(2)}) copy-start(f32[1,512,512]{2,1,0:T(8,128)} %param.4) | copy-start | bytes 3145732
  6.3 22.9 %collective-permute-start.1 = (f32[256,512]{1,0:T(8,128)S(1)}, f32[256,512]{1,0:T(8,128)S(1)}, u32[]{:S(2)}, u32[]{:S(2)}) collective-permute-start(f32[256,512]{1,0:T(8,128)S(1)} %get-tuple-element.32), channel_id=1, source_target_pairs={{8,0},{12,4},{16,8},{20,12},{24,16},{28,20},{0,24},{4,28},{40,32},... | collective-permute-start | bytes 1572872 | tf_op jit(solution)/shard_map/T_row/ppermute | solution.py:27
  9.2 20.4 %collective-permute-start.3 = (f32[256,512]{1,0:T(8,128)S(1)}, f32[256,512]{1,0:T(8,128)S(1)}, u32[]{:S(2)}, u32[]{:S(2)}) collective-permute-start(f32[256,512]{1,0:T(8,128)S(1)} %get-tuple-element.32), channel_id=1, source_target_pairs={{24,0},{28,4},{0,8},{4,12},{8,16},{12,20},{16,24},{20,28},{56,32},... | collective-permute-start | bytes 1572872 | tf_op jit(solution)/shard_map/T_row/ppermute | solution.py:27
  11.5 17.6 %collective-permute-start.9 = (f32[136,512]{1,0:T(8,128)S(1)}, f32[136,512]{1,0:T(8,128)S(1)}, u32[]{:S(2)}, u32[]{:S(2)}) collective-permute-start(f32[136,512]{1,0:T(8,128)S(1)} %get-tuple-element.34), channel_id=1, source_target_pairs={{24,0},{28,4},{0,8},{4,12},{8,16},{12,20},{16,24},{20,28},{56,32},... | collective-permute-start | bytes 835592 | tf_op jit(solution)/shard_map/T_row/ppermute | solution.py:27
  11.6 17.6 %collective-permute-start.6 = (f32[136,512]{1,0:T(8,128)S(1)}, f32[136,512]{1,0:T(8,128)S(1)}, u32[]{:S(2)}, u32[]{:S(2)}) collective-permute-start(f32[136,512]{1,0:T(8,128)S(1)} %get-tuple-element.34), channel_id=1, source_target_pairs={{8,0},{12,4},{16,8},{20,12},{24,16},{28,20},{0,24},{4,28},{40,32},... | collective-permute-start | bytes 835592 | tf_op jit(solution)/shard_map/T_row/ppermute | solution.py:27
  29.2 9.5 %collective-permute-start.7 = (f32[200,512]{1,0:T(8,128)S(1)}, f32[200,512]{1,0:T(8,128)S(1)}, u32[]{:S(2)}, u32[]{:S(2)}) collective-permute-start(f32[200,512]{1,0:T(8,128)S(1)} %pad_maximum_fusion), channel_id=1, source_target_pairs={{8,0},{12,4},{16,8},{20,12},{24,16},{28,20},{0,24},{4,28},{40,32},... | collective-permute-start | bytes 1228808 | tf_op jit(solution)/shard_map/T_row/ppermute | solution.py:27
  29.7 11.5 %collective-permute-start.10 = (f32[192,512]{1,0:T(8,128)S(1)}, f32[192,512]{1,0:T(8,128)S(1)}, u32[]{:S(2)}, u32[]{:S(2)}) collective-permute-start(f32[192,512]{1,0:T(8,128)S(1)} %pad_maximum_fusion.1), channel_id=1, source_target_pairs={{24,0},{28,4},{0,8},{4,12},{8,16},{12,20},{16,24},{20,28},{56,32},... | collective-permute-start | bytes 1179656 | tf_op jit(solution)/shard_map/T_row/ppermute | solution.py:27
  30.9 11.6 %collective-permute-start.2 = (f32[256,512]{1,0:T(8,128)S(1)}, f32[256,512]{1,0:T(8,128)S(1)}, u32[]{:S(2)}, u32[]{:S(2)}) collective-permute-start(f32[256,512]{1,0:T(8,128)S(1)} %collective-permute-done.1.refs_0_), channel_id=1, source_target_pairs={{4,0},{0,4},{12,8},{8,12},{20,16},{16,20},{28,24},{24,28},{36,32},... | collective-permute-start | bytes 1572872 | tf_op jit(solution)/shard_map/T_row/ppermute | solution.py:27
  33.0 10.0 %collective-permute-start.4 = (f32[256,512]{1,0:T(8,128)S(1)}, f32[256,512]{1,0:T(8,128)S(1)}, u32[]{:S(2)}, u32[]{:S(2)}) collective-permute-start(f32[256,512]{1,0:T(8,128)S(1)} %collective-permute-done.3.refs_2_), channel_id=1, source_target_pairs={{4,0},{0,4},{12,8},{8,12},{20,16},{16,20},{28,24},{24,28},{36,32},... | collective-permute-start | bytes 1572872 | tf_op jit(solution)/shard_map/T_row/ppermute | solution.py:27
  38.7 5.1 %collective-permute-start.8 = (f32[200,512]{1,0:T(8,128)S(1)}, f32[200,512]{1,0:T(8,128)S(1)}, u32[]{:S(2)}, u32[]{:S(2)}) collective-permute-start(f32[200,512]{1,0:T(8,128)S(1)} %collective-permute-done.7.refs_4_), channel_id=1, source_target_pairs={{4,0},{0,4},{12,8},{8,12},{20,16},{16,20},{28,24},{24,28},{36,32},... | collective-permute-start | bytes 1228808 | tf_op jit(solution)/shard_map/T_row/ppermute | solution.py:27
  41.2 2.6 %collective-permute-start.11 = (f32[192,512]{1,0:T(8,128)S(1)}, f32[192,512]{1,0:T(8,128)S(1)}, u32[]{:S(2)}, u32[]{:S(2)}) collective-permute-start(f32[192,512]{1,0:T(8,128)S(1)} %collective-permute-done.10.refs_6_), channel_id=1, source_target_pairs={{4,0},{0,4},{12,8},{8,12},{20,16},{16,20},{28,24},{24,28},{36,32},... | collective-permute-start | bytes 1179656 | tf_op jit(solution)/shard_map/T_row/ppermute | solution.py:27
  42.5 4.9 %collective-permute-start.12 = (f32[136,512]{1,0:T(8,128)S(1)}, f32[136,512]{1,0:T(8,128)S(1)}, u32[]{:S(2)}, u32[]{:S(2)}) collective-permute-start(f32[136,512]{1,0:T(8,128)S(1)} %collective-permute-done.6.refs_0_), channel_id=1, source_target_pairs={{4,0},{0,4},{12,8},{8,12},{20,16},{16,20},{28,24},{24,28},{36,32},... | collective-permute-start | bytes 835592 | tf_op jit(solution)/shard_map/T_row/ppermute | solution.py:27
  42.5 4.9 %collective-permute-start.13 = (f32[136,512]{1,0:T(8,128)S(1)}, f32[136,512]{1,0:T(8,128)S(1)}, u32[]{:S(2)}, u32[]{:S(2)}) collective-permute-start(f32[136,512]{1,0:T(8,128)S(1)} %collective-permute-done.9.refs_2_), channel_id=1, source_target_pairs={{4,0},{0,4},{12,8},{8,12},{20,16},{16,20},{28,24},{24,28},{36,32},... | collective-permute-start | bytes 835592 | tf_op jit(solution)/shard_map/T_row/ppermute | solution.py:27
  47.3 8.4 %copy-start.2 = (f32[512,512]{1,0:T(8,128)S(1)}, f32[512,512]{1,0:T(8,128)}, u32[]{:S(2)}) copy-start(f32[512,512]{1,0:T(8,128)} %estimate.1) | copy-start | bytes 3145732
  53.8 6.6 %collective-permute-start.14 = (f32[136,512]{1,0:T(8,128)S(1)}, f32[136,512]{1,0:T(8,128)S(1)}, u32[]{:S(2)}, u32[]{:S(2)}) collective-permute-start(f32[136,512]{1,0:T(8,128)S(1)} %get-tuple-element.38), channel_id=1, source_target_pairs={{96,64},{100,68},{104,72},{108,76},{112,80},{116,84},{120,88},{124... | collective-permute-start | bytes 835592 | tf_op jit(solution)/shard_map/T_z/ppermute | solution.py:27
  54.4 15.0 %collective-permute-start.20 = (f32[256,512]{1,0:T(8,128)S(1)}, f32[256,512]{1,0:T(8,128)S(1)}, u32[]{:S(2)}, u32[]{:S(2)}) collective-permute-start(f32[256,512]{1,0:T(8,128)S(1)} %get-tuple-element.51), channel_id=1, source_target_pairs={{32,0},{36,4},{40,8},{44,12},{48,16},{52,20},{56,24},{60,28},{33,1... | collective-permute-start | bytes 1572872 | tf_op jit(solution)/shard_map/T_z/ppermute | solution.py:27
  60.4 4.2 %collective-permute-start.15 = (f32[136,512]{1,0:T(8,128)S(1)}, f32[136,512]{1,0:T(8,128)S(1)}, u32[]{:S(2)}, u32[]{:S(2)}) collective-permute-start(f32[136,512]{1,0:T(8,128)S(1)} %collective-permute-done.14.mine), channel_id=1, source_target_pairs={{4,0},{0,4},{12,8},{8,12},{20,16},{16,20},{28,24},{24,28},{36,32},... | collective-permute-start | bytes 835592 | tf_op jit(solution)/shard_map/T_z/ppermute | solution.py:27
  63.3 12.1 %collective-permute-start.22 = (f32[136,512]{1,0:T(8,128)S(1)}, f32[136,512]{1,0:T(8,128)S(1)}, u32[]{:S(2)}, u32[]{:S(2)}) collective-permute-start(f32[136,512]{1,0:T(8,128)S(1)} %get-tuple-element.38), channel_id=1, source_target_pairs={{32,0},{36,4},{40,8},{44,12},{48,16},{52,20},{56,24},{60,28},{33,1... | collective-permute-start | bytes 835592 | tf_op jit(solution)/shard_map/T_z/ppermute | solution.py:27
  66.6 10.1 %collective-permute-start.16 = (f32[136,512]{1,0:T(8,128)S(1)}, f32[136,512]{1,0:T(8,128)S(1)}, u32[]{:S(2)}, u32[]{:S(2)}) collective-permute-start(f32[136,512]{1,0:T(8,128)S(1)} %get-tuple-element.50), channel_id=1, source_target_pairs={{64,32},{68,36},{72,40},{76,44},{80,48},{84,52},{88,56},{92,60},{6... | collective-permute-start | bytes 835592 | tf_op jit(solution)/shard_map/T_z/ppermute | solution.py:27
  67.3 13.4 %collective-permute-start.18 = (f32[136,512]{1,0:T(8,128)S(1)}, f32[136,512]{1,0:T(8,128)S(1)}, u32[]{:S(2)}, u32[]{:S(2)}) collective-permute-start(f32[136,512]{1,0:T(8,128)S(1)} %get-tuple-element.50), channel_id=1, source_target_pairs={{64,0},{68,4},{72,8},{76,12},{80,16},{84,20},{88,24},{92,28},{65,1... | collective-permute-start | bytes 835592 | tf_op jit(solution)/shard_map/T_z/ppermute | solution.py:27
  69.5 12.2 %collective-permute-start.21 = (f32[256,512]{1,0:T(8,128)S(1)}, f32[256,512]{1,0:T(8,128)S(1)}, u32[]{:S(2)}, u32[]{:S(2)}) collective-permute-start(f32[256,512]{1,0:T(8,128)S(1)} %collective-permute-done.20.lead), channel_id=1, source_target_pairs={{4,0},{0,4},{12,8},{8,12},{20,16},{16,20},{28,24},{24,28},{36,32},... | collective-permute-start | bytes 1572872 | tf_op jit(solution)/shard_map/T_z/ppermute | solution.py:27
  75.5 6.2 %collective-permute-start.23 = (f32[136,512]{1,0:T(8,128)S(1)}, f32[136,512]{1,0:T(8,128)S(1)}, u32[]{:S(2)}, u32[]{:S(2)}) collective-permute-start(f32[136,512]{1,0:T(8,128)S(1)} %collective-permute-done.22.first), channel_id=1, source_target_pairs={{4,0},{0,4},{12,8},{8,12},{20,16},{16,20},{28,24},{24,28},{36,32},... | collective-permute-start | bytes 835592 | tf_op jit(solution)/shard_map/T_z/ppermute | solution.py:27
  76.7 5.0 %collective-permute-start.17 = (f32[136,512]{1,0:T(8,128)S(1)}, f32[136,512]{1,0:T(8,128)S(1)}, u32[]{:S(2)}, u32[]{:S(2)}) collective-permute-start(f32[136,512]{1,0:T(8,128)S(1)} %collective-permute-done.16.near), channel_id=1, source_target_pairs={{4,0},{0,4},{12,8},{8,12},{20,16},{16,20},{28,24},{24,28},{36,32},... | collective-permute-start | bytes 835592 | tf_op jit(solution)/shard_map/T_z/ppermute | solution.py:27
  80.7 2.2 %collective-permute-start.19 = (f32[136,512]{1,0:T(8,128)S(1)}, f32[136,512]{1,0:T(8,128)S(1)}, u32[]{:S(2)}, u32[]{:S(2)}) collective-permute-start(f32[136,512]{1,0:T(8,128)S(1)} %collective-permute-done.18.far), channel_id=1, source_target_pairs={{4,0},{0,4},{12,8},{8,12},{20,16},{16,20},{28,24},{24,28},{36,32},... | collective-permute-start | bytes 835592 | tf_op jit(solution)/shard_map/T_z/ppermute | solution.py:27
  86.8 2.0 %collective-permute-start.24 = (f32[256,512]{1,0:T(8,128)S(1)}, f32[256,512]{1,0:T(8,128)S(1)}, u32[]{:S(2)}, u32[]{:S(2)}) collective-permute-start(f32[256,512]{1,0:T(8,128)S(1)} %get-tuple-element.57), channel_id=1, source_target_pairs={{4,0},{0,4},{12,8},{8,12},{20,16},{16,20},{28,24},{24,28},{36,32},... | collective-permute-start | bytes 1572872 | tf_op jit(solution)/shard_map/T_reduce/ppermute | solution.py:27
  115.9 4.2 %collective-permute-start.25 = (f32[256,512]{1,0:T(8,128)S(1)}, f32[256,512]{1,0:T(8,128)S(1)}, u32[]{:S(2)}, u32[]{:S(2)}) collective-permute-start(f32[256,512]{1,0:T(8,128)S(1)} %bitcast.4), channel_id=1, source_target_pairs={{4,0},{0,4},{12,8},{8,12},{20,16},{16,20},{28,24},{24,28},{36,32},... | collective-permute-start | bytes 1572872 | tf_op jit(solution)/shard_map/T_reduce/ppermute | solution.py:27
